TPU v7x, 32 devices: a whole 2x2x4 slice. The times are simulated.
32 devices in a mesh: rep: 8 (over y, x, core), sp: 4 (over z).
Axes of the slice: x: 2, y: 2, z: 4, core: 2. Of those that a mesh axis runs over, the one named last changes fastest.
Arguments:
- field: bfloat16 [8, 128, 100, 128], P('rep', 'sp'), may hold values from -6 to 6
- send_blocks: int32 [4, 4, 8], P('sp'), may hold values from 0 to 31
- send_count: int32 [4, 4], P('sp'), may hold values from 1 to 8, as said below
- regrid_weights: bfloat16 [32, 8, 128, 128], P('sp'), may hold values from -0.1875 to 0.1875
- tile_slot: int32 [32, 8], P('sp'), may hold values from 0 to 31
- edge_inputs: bfloat16 [12288, 1536], P(('rep', 'sp')), may hold values from -6 to 6
- cotangent: bfloat16 [12288, 512], P(('rep', 'sp')), may hold values from -0.15625 to 0.15625
Outputs:
- hidden: bfloat16 [8, 32, 100, 128], P('rep', 'sp')
- weight_grad: float32 [1536, 512], P(('rep', 'sp'))
Inputs may be any that keep to these rules, and one draw needn't show every extreme that they name: `send_count`: every count is at most 8, and some pair of shards has exactly 8 in every draw.
All inputs are finite; a program needn't handle non-finite values.
Results may differ from a plain program's by a relative error of at most 0.001.
Values may be sent and summed in bfloat16 or wider, within the bound.
No kernel may reach another device: no remote copies, remote signals or barrier semaphores. Data moves between devices by JAX's collectives and lax.ppermute only.
A program may use at most 64 MiB of HBM per device.

v0:
```python
import jax
import jax.numpy as jnp
from jax import lax
from jax.sharding import PartitionSpec as P


def body(field, send_blocks, send_count, regrid_weights, tile_slot, edge_inputs, cotangent):
    sample = field[0]
    own_lists = send_blocks[0]
    shards = own_lists.shape[0]
    slots_each = own_lists.shape[1]
    channels = sample.shape[1]
    cells = sample.shape[2]
    alive = jnp.arange(slots_each, dtype=jnp.int32)[None, :] < send_count[0][:, None]
    outgoing = jnp.where(alive[:, :, None, None], sample[own_lists], jnp.zeros((), jnp.bfloat16))
    incoming = lax.all_to_all(outgoing, "sp", split_axis=0, concat_axis=0, tiled=True)
    block_pool = incoming.reshape(shards * slots_each, channels, cells)
    picked = block_pool[tile_slot]
    hidden = jnp.einsum(
        "tbcx,tbxn->tcn", picked, regrid_weights, preferred_element_type=jnp.float32
    )
    hidden = hidden.astype(jnp.bfloat16)[None]
    partial_value = lax.psum_scatter(
        lax.dot_general(
            edge_inputs, cotangent, (((0,), (0,)), ((), ())), preferred_element_type=jnp.float32
        ),
        "rep",
        scatter_dimension=0,
        tiled=True,
    )
    weight_grad = lax.psum_scatter(partial_value, "sp", scatter_dimension=0, tiled=True)
    return (hidden, weight_grad)


def solution(mesh):
    in_specs = (
        P("rep", "sp", None, None),
        P("sp", None, None),
        P("sp", None),
        P("sp", None, None, None),
        P("sp", None),
        P(("rep", "sp"), None),
        P(("rep", "sp"), None),
    )
    out_specs = (P("rep", "sp", None, None), P(("rep", "sp"), None))
    return jax.shard_map(body, mesh=mesh, in_specs=in_specs, out_specs=out_specs, check_vma=False)
```

profile of v0, /device:TPU:0, one launch (start us, length us, event | category | flops | bytes accessed | tf_op | source)
XLA Modules:
  0.0 90.9 jit_solution(5322619930155869061)
XLA Ops:
  7.2 0.0 copy-start
  7.2 0.0 reduce-scatter.3.cloned.1.call-start
  7.2 4.1 %fusion.2 = f32[1536,512]{1,0:T(8,128)} fusion(bf16[384,1536]{1,0:T(8,128)(2,1)} %param.12, bf16[384,512]{1,0:T(8,128)(2,1)} %param.13), kind=kOutput, calls=%fused_computation.12 | convolution fusion | flops 603979776 | bytes 4718592 | tf_op jit(solution)/shard_map/dot_general | solution.py:24
  11.4 0.0 copy-start.3
  11.4 0.0 copy-start.1
  11.4 0.0 reduce-scatter.3.cloned.1.call-update
  11.4 0.7 copy-done.3
  12.1 0.0 copy-start.4
  12.1 0.1 reshape.62
  12.1 0.4 copy-done.1
  12.5 1.2 %copy.19 = bf16[1,32,100,128]{3,2,1,0:T(8,128)(2,1)} copy(bf16[1,32,100,128]{3,1,2,0:T(8,128)(2,1)S(1)} %copy-done.1) | data formatting | bytes 1638400 | tf_op args[0]
  13.8 1.9 %gather_fusion = bf16[32,100,128]{2,1,0:T(8,128)(2,1)S(1)} fusion(bf16[32,100,128]{2,1,0:T(8,128)(2,1)} %bitcast.27, s32[1024]{0:T(1024)S(1)} %pad_clamp_fusion.1), kind=kCustom, calls=%fused_computation | custom fusion | bytes 1638528 | tf_op jit(solution)/shard_map/gather | solution.py:15
  15.6 0.0 copy-done.4
  15.7 0.1 iota_compare_fusion
  15.7 0.0 copy-start.2
  15.7 1.0 %copy_select_fusion = bf16[4,8,100,128]{3,1,2,0:T(8,128)(2,1)} fusion(bf16[4,8,100,128]{3,2,1,0:T(8,128)(2,1)S(1)} %bitcast.26, pred[4,8]{1,0:T(4,128)(4,1)S(1)} %iota_compare_fusion), kind=kLoop, calls=%fused_computation.6 | loop fusion | flops 409600 | bytes 1638432 | tf_op jit(solution)/shard_map/jit(_where)/select_n | solution.py:15
  16.8 6.3 %all-to-all-start = ((bf16[4,8,100,128]{3,1,2,0:T(8,128)(2,1)}), bf16[4,8,100,128]{3,1,2,0:T(8,128)(2,1)}, u32[]{:S(2)}, u32[]{:S(2)}) async-start(bf16[4,8,100,128]{3,1,2,0:T(8,128)(2,1)} %copy_select_fusion), calls=%async_computation | async-start | bytes 1638400 | tf_op jit(solution)/shard_map/all_to_all | solution.py:16
  23.1 0.0 reduce-scatter.5.cloned.1.call-start
  23.1 37.2 %reduce-scatter.3.cloned.1.call-done = f32[192,512]{1,0:T(8,128)} async-done(((f32[1536,512]{1,0:T(8,128)}), f32[192,512]{1,0:T(8,128)}) %reduce-scatter.3.cloned.1.call-update) | async-done | bytes 393232 | tf_op jit(solution)/shard_map/reduce_scatter | solution.py:23
  60.3 0.0 reduce-scatter.5.cloned.1.call-update
  60.4 0.0 copy-done.2
  60.4 0.1 reshape.70
  60.5 0.0 all-to-all-done
  60.5 1.3 %copy.14 = bf16[4,8,100,128]{3,2,1,0:T(8,128)(2,1)S(1)} copy(bf16[4,8,100,128]{3,1,2,0:T(8,128)(2,1)} %all-to-all-done) | data formatting | bytes 1638400 | tf_op jit(solution)/shard_map/all_to_all | solution.py:16
  61.8 2.0 %gather_fusion.1 = bf16[64,100,128]{2,1,0:T(8,128)(2,1)} fusion(bf16[32,100,128]{2,1,0:T(8,128)(2,1)S(1)} %bitcast.24, s32[1024]{0:T(1024)S(1)} %pad_clamp_fusion), kind=kCustom, calls=%fused_computation.1 | custom fusion | bytes 3277056 | tf_op jit(solution)/shard_map/gather | solution.py:18
  63.8 0.0 copy-done
  63.8 2.1 %fusion.1 = bf16[1,8,100,128]{3,2,1,0:T(8,128)(2,1)S(1)} fusion(bf16[8,8,100,128]{3,2,1,0:T(8,128)(2,1)} %bitcast.25, bf16[8,8,128,128]{3,2,1,0:T(8,128)(2,1)S(1)} %copy-done), kind=kOutput, calls=%fused_computation.4 | convolution fusion | flops 209817600 | bytes 3940352 | tf_op jit(solution)/shard_map/tbcx,tbxn->tcn/dot_general | solution.py:19
  65.9 0.7 copy.15
  66.6 17.4 %reduce-scatter.5.cloned.1.call-done = f32[48,512]{1,0:T(8,128)} async-done(((f32[192,512]{1,0:T(8,128)}), f32[48,512]{1,0:T(8,128)}) %reduce-scatter.5.cloned.1.call-update) | async-done | bytes 98320 | tf_op jit(solution)/shard_map/reduce_scatter | solution.py:31
  (4 shorter events, 0.0 us)
Async XLA Ops:
  7.2 56.6 %copy-start = (bf16[8,8,128,128]{3,2,1,0:T(8,128)(2,1)S(1)}, bf16[8,8,128,128]{3,2,1,0:T(8,128)(2,1)}, u32[]{:S(2)}) copy-start(bf16[8,8,128,128]{3,2,1,0:T(8,128)(2,1)} %param.10) | copy-start | bytes 6291460
  7.2 53.2 %reduce-scatter.3.cloned.1.call-start = ((), (), s32[]{:S(2)}) async-start(), calls=%async_computation.3 | async-start | bytes 3538944 | tf_op jit(solution)/shard_map/reduce_scatter | solution.py:23
  11.4 0.7 copy-start.3
  11.4 1.2 %copy-start.1 = (bf16[1,32,100,128]{3,1,2,0:T(8,128)(2,1)S(1)}, bf16[1,32,100,128]{3,1,2,0:T(8,128)(2,1)}, u32[]{:S(2)}) copy-start(bf16[1,32,100,128]{3,1,2,0:T(8,128)(2,1)} %param.7) | copy-start | bytes 2457604
  12.1 3.6 %copy-start.4 = (s32[1,4]{1,0:T(1,128)S(1)}, s32[1,4]{1,0:T(1,128)}, u32[]{:S(2)}) copy-start(s32[1,4]{1,0:T(1,128)} %param.9) | copy-start | bytes 52
  15.7 44.6 %copy-start.2 = (s32[8,8]{1,0:T(8,128)S(1)}, s32[8,8]{1,0:T(8,128)}, u32[]{:S(2)}) copy-start(s32[8,8]{1,0:T(8,128)} %param.11) | copy-start | bytes 772
  16.8 43.7 %all-to-all-start = ((bf16[4,8,100,128]{3,1,2,0:T(8,128)(2,1)}), bf16[4,8,100,128]{3,1,2,0:T(8,128)(2,1)}, u32[]{:S(2)}, u32[]{:S(2)}) async-start(bf16[4,8,100,128]{3,1,2,0:T(8,128)(2,1)} %copy_select_fusion), calls=%async_computation | async-start | bytes 1638400 | tf_op jit(solution)/shard_map/all_to_all | solution.py:16
  23.1 60.9 %reduce-scatter.5.cloned.1.call-start = ((), (), s32[]{:S(2)}) async-start(), calls=%async_computation.4 | async-start | bytes 491520 | tf_op jit(solution)/shard_map/reduce_scatter | solution.py:31
Sparse Core Ops, SparseCore 0:
  11.5 48.7 reduce-scatter.2
  63.2 20.7 reduce-scatter.4
where the time goes:
time: 91.2 us; the launch traced here: 90.9 us
  waiting for transfers between devices  54.7 us (60%)
  between operations  14.1 us (15%)
  local copies, waits for them, and re-layouts  8.3 us (9%)
  starting transfers between devices  6.39 us (7%)
  matrix products  6.26 us (7%)
  other arithmetic  1.12 us (1%)
    reduce_scatter x1, waiting for transfers between devices, body(): lax.psum_scatter(lax.dot_general(edge_inputs, cotangent, (((0,), (0,)), (...  37.2 us
    reduce_scatter x1, waiting for transfers between devices, body(): lax.psum_scatter(partial_value, 'sp', scatter_dimension=0, tiled=True)  17.4 us
    all_to_all x1, starting transfers between devices, body(): lax.all_to_all(outgoing, 'sp', split_axis=0, concat_axis=0, tiled=True)  6.35 us
    dot_general x1, matrix products, body(): lax.dot_general(edge_inputs, cotangent, (((0,), (0,)), ((), ())), preferr...  4.15 us
    unnamed x12, local copies, waits for them, and re-layouts  3 us
    dot_general x1, matrix products, body(): jnp.einsum('tbcx,tbxn->tcn', picked, regrid_weights, preferred_element_ty...  2.12 us
    gather x1, local copies, waits for them, and re-layouts, body(): picked = block_pool[tile_slot]  1.99 us
    gather x1, local copies, waits for them, and re-layouts, body(): sample[own_lists]  1.87 us
  transfers between devices with their start and end apart: 3, of which 2 were waited for; matrix products, arithmetic and copies ran while one was open for 12% of the time, Pallas kernels for 0%

commit v1 on v0

v1 whole, which is shorter than its diff:
```python
import jax
import jax.numpy as jnp
from jax import lax
from jax.sharding import Mesh, PartitionSpec as P


def body(field, send_blocks, send_count, regrid_weights, tile_slot, edge_inputs, cotangent):
    sample = field[0]
    own_lists = send_blocks[0]
    shards = own_lists.shape[0]
    slots_each = own_lists.shape[1]
    channels = sample.shape[1]
    cells = sample.shape[2]
    groups = lax.axis_size("group")
    alive = jnp.arange(slots_each, dtype=jnp.int32)[None, :] < send_count[0][:, None]
    outgoing = jnp.where(alive[:, :, None, None], sample[own_lists], jnp.zeros((), jnp.bfloat16))
    incoming = lax.all_to_all(outgoing, "sp", split_axis=0, concat_axis=0, tiled=True)

    partial_grad = lax.dot_general(
        edge_inputs, cotangent, (((0,), (0,)), ((), ())), preferred_element_type=jnp.float32
    )
    rows = partial_grad.shape[0] // (groups * 2 * shards)
    hid = partial_grad.shape[1]
    halves = partial_grad.reshape(groups, 2, shards * rows, hid)
    first = lax.axis_index("pair") == 0
    keep = jnp.where(first, halves[:, 0], halves[:, 1])
    give = jnp.where(first, halves[:, 1], halves[:, 0])
    pair_sum = keep + lax.ppermute(give, "pair", [(0, 1), (1, 0)])
    shift = jnp.clip(14.0 - jnp.ceil(jnp.log2(jnp.max(jnp.abs(pair_sum)))), -100.0, 100.0)
    scaled = (pair_sum * jnp.exp2(shift)).astype(jnp.float16)
    scaled = scaled.reshape(groups * shards, rows, hid)
    tag = jnp.full((groups * shards, 1, hid), shift.astype(jnp.float16))
    received = lax.all_to_all(
        jnp.concatenate([scaled, tag], axis=1), ("group", "sp"), split_axis=0, concat_axis=0, tiled=True
    )
    unscale = jnp.exp2(-received[:, rows:, :].astype(jnp.float32))
    weight_grad = jnp.sum(received[:, :rows].astype(jnp.float32) * unscale, axis=0)

    block_pool = incoming.reshape(shards * slots_each, channels, cells)
    picked = block_pool[tile_slot]
    hidden = jnp.einsum(
        "tbcx,tbxn->tcn", picked, regrid_weights, preferred_element_type=jnp.float32
    )
    hidden = hidden.astype(jnp.bfloat16)[None]
    return (hidden, weight_grad)


def solution(mesh):
    split = Mesh(
        mesh.devices.reshape(mesh.shape["rep"] // 2, 2, mesh.shape["sp"]), ("group", "pair", "sp")
    )
    rep = ("group", "pair")
    in_specs = (
        P(rep, "sp", None, None),
        P("sp", None, None),
        P("sp", None),
        P("sp", None, None, None),
        P("sp", None),
        P((*rep, "sp"), None),
        P((*rep, "sp"), None),
    )
    out_specs = (P(rep, "sp", None, None), P((*rep, "sp"), None))
    return jax.shard_map(body, mesh=split, in_specs=in_specs, out_specs=out_specs, check_vma=False)
```

time: 91.2 us -> 72.5 us (0.79)
  waiting for transfers between devices: 54.7 us -> 30.7 us
  other arithmetic: 1.12 us -> 14 us
  between operations: 14.1 us -> 1.48 us
  starting transfers between devices: 6.39 us -> 11.5 us
    reduce_scatter x2 -> x0, waiting for transfers between devices: 54.7 us -> none  [the longest x1 37.2 us: body(): lax.psum_scatter(lax.dot_general(edge_inputs, cotangent, (((0,), (0,)), (...]
    all_to_all x0 -> x1, waiting for transfers between devices: none -> 17.7 us  [body(): lax.all_to_all(jnp.concatenate([scaled, tag], axis=1), ('group', 'sp'), s...]
    all_to_all x1, waiting for transfers between devices: 0.01 us -> 13 us  [body(): lax.all_to_all(outgoing, 'sp', split_axis=0, concat_axis=0, tiled=True)]
    all_to_all x0 -> x1, starting transfers between devices: none -> 4.77 us  [body(): lax.all_to_all(jnp.concatenate([scaled, tag], axis=1), ('group', 'sp'), s...]
    reduce_max x0 -> x1, other arithmetic: none -> 4.66 us  [body(): jnp.max(jnp.abs(pair_sum))]
    select_n x0 -> x1, other arithmetic: none -> 3.5 us  [body(): give = jnp.where(first, halves[:, 1], halves[:, 0])]
    reduce_sum x0 -> x1, other arithmetic: none -> 1.95 us  [body(): jnp.sum(received[:, :rows].astype(jnp.float32) * unscale, axis=0)]
    unnamed x12 -> x14, local copies, waits for them, and re-layouts: 3 us -> 1.06 us
  transfers between devices with their start and end apart: 3 -> 3, of which waited for: 2 -> 2; matrix products, arithmetic and copies ran while one was open for 12% -> 25% of each run, Pallas kernels for 0% -> 0%
where the time goes in v1:
time: 72.5 us; the launch traced here: 72 us
  waiting for transfers between devices  30.7 us (42%)
  other arithmetic  14 us (19%)
  starting transfers between devices  11.5 us (16%)
  local copies, waits for them, and re-layouts  8.11 us (11%)
  matrix products  6.28 us (9%)
  between operations  1.48 us (2%)
    all_to_all x1, waiting for transfers between devices, body(): lax.all_to_all(jnp.concatenate([scaled, tag], axis=1), ('group', 'sp'), s...  17.7 us
    all_to_all x1, waiting for transfers between devices, body(): lax.all_to_all(outgoing, 'sp', split_axis=0, concat_axis=0, tiled=True)  13 us
    all_to_all x1, starting transfers between devices, body(): lax.all_to_all(outgoing, 'sp', split_axis=0, concat_axis=0, tiled=True)  6.19 us
    all_to_all x1, starting transfers between devices, body(): lax.all_to_all(jnp.concatenate([scaled, tag], axis=1), ('group', 'sp'), s...  4.77 us
    reduce_max x1, other arithmetic, body(): jnp.max(jnp.abs(pair_sum))  4.66 us
    dot_general x1, matrix products, body(): lax.dot_general(edge_inputs, cotangent, (((0,), (0,)), ((), ())), preferr...  4.16 us
    select_n x1, other arithmetic, body(): give = jnp.where(first, halves[:, 1], halves[:, 0])  3.5 us
    select_n x1, other arithmetic, body(): jnp.where(alive[:, :, None, None], sample[own_lists], jnp.zeros((), jnp.b...  2.2 us
  transfers between devices with their start and end apart: 3, of which 2 were waited for; matrix products, arithmetic and copies ran while one was open for 25% of the time, Pallas kernels for 0%

profile of v1, /device:TPU:0, one launch (start us, length us, event | category | flops | bytes accessed | tf_op | source)
XLA Modules:
  0.0 72.0 jit_solution(3346583591322920819)
XLA Ops:
  0.6 0.0 copy-start
  0.6 4.2 %fusion.2 = f32[1536,512]{1,0:T(8,128)} fusion(bf16[384,1536]{1,0:T(8,128)(2,1)} %param.12, bf16[384,512]{1,0:T(8,128)(2,1)} %param.13), kind=kOutput, calls=%fused_computation.20 | convolution fusion | flops 603979776 | bytes 4718592 | tf_op jit(solution)/shard_map/dot_general | solution.py:19
  4.8 0.0 copy-start.2
  4.8 3.5 %select_bitcast_fusion = f32[4,192,512]{2,1,0:T(8,128)} fusion(f32[4,2,192,512]{3,2,1,0:T(8,128)} %bitcast.47, pred[]{:T(512)S(6)} %eq.3), kind=kLoop, calls=%fused_computation.8 | loop fusion | flops 393216 | bytes 4718593 | tf_op jit(solution)/shard_map/jit(_where)/select_n | solution.py:27
  8.3 0.5 collective-permute-start
  8.8 0.0 copy-done.2
  8.8 0.3 copy.57
  9.1 0.0 copy-done.4
  9.2 0.1 reshape.74
  9.2 1.6 %gather_fusion = bf16[32,100,128]{2,1,0:T(8,128)(2,1)} fusion(bf16[32,100,128]{2,1,0:T(8,128)(2,1)S(1)} %bitcast.51, s32[1024]{0:T(1024)S(1)} %pad_clamp_fusion.1), kind=kCustom, calls=%fused_computation | custom fusion | bytes 1638528 | tf_op jit(solution)/shard_map/gather | solution.py:16
  10.8 0.0 copy-done.5
  10.8 0.1 iota_compare_fusion
  10.9 2.2 %copy_select_fusion = bf16[4,8,100,128]{3,1,2,0:T(8,128)(2,1)} fusion(bf16[4,8,100,128]{3,2,1,0:T(8,128)(2,1)} %bitcast.52, pred[4,8]{1,0:T(4,128)(4,1)S(1)} %iota_compare_fusion), kind=kLoop, calls=%fused_computation.13 | loop fusion | flops 409600 | bytes 1638432 | tf_op jit(solution)/shard_map/jit(_where)/select_n | solution.py:16
  13.1 6.2 %all-to-all-start = ((bf16[4,8,100,128]{3,1,2,0:T(8,128)(2,1)}), bf16[4,8,100,128]{3,1,2,0:T(8,128)(2,1)S(1)}, u32[]{:S(2)}, u32[]{:S(2)}) async-start(bf16[4,8,100,128]{3,1,2,0:T(8,128)(2,1)} %copy_select_fusion), calls=%async_computation | async-start | bytes 1638400 | tf_op jit(solution)/shard_map/all_to_all | solution.py:17
  19.3 0.0 collective-permute-done
  19.3 4.7 %abs_reduce_fusion = (f32[]{:T(128)}, f32[4,192,512]{2,1,0:T(8,128)}) fusion(f32[4,192,512]{2,1,0:T(8,128)} %collective-permute-done, f32[4,2,192,512]{3,2,1,0:T(8,128)} %bitcast.48, pred[]{:T(512)S(6)} %eq.3), kind=kLoop, calls=%fused_computation.7 | loop fusion | flops 1572863 | bytes 6291461 | tf_op jit(solution)/shard_map/reduce_max | solution.py:29
  24.7 1.6 %multiply_convert_fusion = f16[4,192,512]{2,1,0:T(8,128)(2,1)S(1)} fusion(f32[4,192,512]{2,1,0:T(8,128)} %get-tuple-element.15, f32[]{:T(128)S(6)} %exp2.16), kind=kLoop, calls=%fused_computation.6 | loop fusion | flops 786432 | bytes 2359300 | tf_op jit(solution)/shard_map/convert_element_type | solution.py:30
  26.3 0.0 copy-start.3
  26.3 1.1 %concatenate.3 = f16[16,49,512]{2,1,0:T(8,128)(2,1)} pad(f16[16,48,512]{2,1,0:T(8,128)(2,1)S(1)} %bitcast.53, f16[]{:T(256)S(6)} %convert_element_type.17), padding=0_0x0_1x0_0 | pad | bytes 1589250 | tf_op jit(solution)/shard_map/concatenate | solution.py:34
  27.4 13.0 %all-to-all-done = bf16[4,8,100,128]{3,1,2,0:T(8,128)(2,1)S(1)} async-done(((bf16[4,8,100,128]{3,1,2,0:T(8,128)(2,1)}), bf16[4,8,100,128]{3,1,2,0:T(8,128)(2,1)S(1)}, u32[]{:S(2)}, u32[]{:S(2)}) %all-to-all-start) | async-done | bytes 819232 | tf_op jit(solution)/shard_map/all_to_all | solution.py:17
  40.5 4.8 %all-to-all-start.1 = ((f16[16,49,512]{2,1,0:T(8,128)(2,1)}), f16[16,49,512]{2,1,0:T(8,128)(2,1)}, u32[]{:S(2)}, u32[]{:S(2)}) async-start(f16[16,49,512]{2,1,0:T(8,128)(2,1)} %concatenate.3), calls=%async_computation.1 | async-start | bytes 1835008 | tf_op jit(solution)/shard_map/all_to_all | solution.py:33
  45.2 0.0 copy-done.3
  45.3 0.1 reshape.82
  45.3 0.0 copy-done.1
  45.3 1.3 %copy.45 = bf16[4,8,100,128]{3,2,1,0:T(8,128)(2,1)S(1)} copy(bf16[4,8,100,128]{3,1,2,0:T(8,128)(2,1)} %copy-done.1) | data formatting | bytes 1638400 | tf_op jit(solution)/shard_map/all_to_all | solution.py:17
  46.6 2.0 %gather_fusion.1 = bf16[64,100,128]{2,1,0:T(8,128)(2,1)} fusion(bf16[32,100,128]{2,1,0:T(8,128)(2,1)S(1)} %bitcast.49, s32[1024]{0:T(1024)S(1)} %pad_clamp_fusion), kind=kCustom, calls=%fused_computation.1 | custom fusion | bytes 3277056 | tf_op jit(solution)/shard_map/gather | solution.py:40
  48.6 0.0 copy-done
  48.6 2.1 %fusion.1 = bf16[1,8,100,128]{3,2,1,0:T(8,128)(2,1)S(1)} fusion(bf16[8,8,100,128]{3,2,1,0:T(8,128)(2,1)} %bitcast.50, bf16[8,8,128,128]{3,2,1,0:T(8,128)(2,1)S(1)} %copy-done), kind=kOutput, calls=%fused_computation.11 | convolution fusion | flops 209817600 | bytes 3940352 | tf_op jit(solution)/shard_map/tbcx,tbxn->tcn/dot_general | solution.py:41
  50.7 0.7 copy.49
  51.4 17.7 %all-to-all-done.1 = f16[16,49,512]{2,1,0:T(8,128)(2,1)} async-done(((f16[16,49,512]{2,1,0:T(8,128)(2,1)}), f16[16,49,512]{2,1,0:T(8,128)(2,1)}, u32[]{:S(2)}, u32[]{:S(2)}) %all-to-all-start.1) | async-done | bytes 802848 | tf_op jit(solution)/shard_map/all_to_all | solution.py:33
  69.1 0.9 %slice.25 = f16[16,1,512]{2,1,0:T(2,128)(2,1)S(1)} slice(f16[16,49,512]{2,1,0:T(8,128)(2,1)} %all-to-all-done.1), slice={[0:16], [48:49], [0:512]} | slice | bytes 32768 | tf_op jit(solution)/shard_map/slice | solution.py:36
  70.1 1.9 %multiply_reduce_fusion = f32[48,512]{1,0:T(8,128)} fusion(f16[16,49,512]{2,1,0:T(8,128)(2,1)} %all-to-all-done.1, f32[16,512]{1,0:T(8,128)S(1)} %exponential_bitcast_fusion), kind=kLoop, calls=%fused_computation.5 | loop fusion | flops 1155072 | bytes 917504 | tf_op jit(solution)/shard_map/reduce_sum | solution.py:37
  (8 shorter events, 0.0 us)
Async XLA Ops:
  0.6 48.0 %copy-start = (bf16[8,8,128,128]{3,2,1,0:T(8,128)(2,1)S(1)}, bf16[8,8,128,128]{3,2,1,0:T(8,128)(2,1)}, u32[]{:S(2)}) copy-start(bf16[8,8,128,128]{3,2,1,0:T(8,128)(2,1)} %param.10) | copy-start | bytes 6291460
  4.8 4.0 %copy-start.2 = (bf16[1,32,100,128]{3,1,2,0:T(8,128)(2,1)S(1)}, bf16[1,32,100,128]{3,1,2,0:T(8,128)(2,1)}, u32[]{:S(2)}) copy-start(bf16[1,32,100,128]{3,1,2,0:T(8,128)(2,1)} %param.7) | copy-start | bytes 2457604
  8.3 0.8 %copy-start.4 = (s32[1,4,8]{2,1,0:T(4,128)S(1)}, s32[1,4,8]{2,1,0:T(4,128)}, u32[]{:S(2)}) copy-start(s32[1,4,8]{2,1,0:T(4,128)} %param.8) | copy-start | bytes 388
  8.3 2.5 %copy-start.5 = (s32[1,4]{1,0:T(1,128)S(1)}, s32[1,4]{1,0:T(1,128)}, u32[]{:S(2)}) copy-start(s32[1,4]{1,0:T(1,128)} %param.9) | copy-start | bytes 52
  8.3 11.0 %collective-permute-start = (f32[4,192,512]{2,1,0:T(8,128)}, f32[4,192,512]{2,1,0:T(8,128)}, u32[]{:S(2)}, u32[]{:S(2)}) collective-permute-start(f32[4,192,512]{2,1,0:T(8,128)} %select_bitcast_fusion), channel_id=1, source_target_pairs={{0,4},{4,0},{1,5},{5,1},{2,6},{6,2},{3,7},{7,3},{8,12},{12,8},{9,1... | collective-permute-start | bytes 4718600 | tf_op jit(solution)/shard_map/ppermute | solution.py:28
  13.1 27.3 %all-to-all-start = ((bf16[4,8,100,128]{3,1,2,0:T(8,128)(2,1)}), bf16[4,8,100,128]{3,1,2,0:T(8,128)(2,1)S(1)}, u32[]{:S(2)}, u32[]{:S(2)}) async-start(bf16[4,8,100,128]{3,1,2,0:T(8,128)(2,1)} %copy_select_fusion), calls=%async_computation | async-start | bytes 1638400 | tf_op jit(solution)/shard_map/all_to_all | solution.py:17
  26.3 18.9 %copy-start.3 = (s32[8,8]{1,0:T(8,128)S(1)}, s32[8,8]{1,0:T(8,128)}, u32[]{:S(2)}) copy-start(s32[8,8]{1,0:T(8,128)} %param.11) | copy-start | bytes 772
  40.4 4.9 %copy-start.1 = (bf16[4,8,100,128]{3,1,2,0:T(8,128)(2,1)}, bf16[4,8,100,128]{3,1,2,0:T(8,128)(2,1)S(1)}, u32[]{:S(2)}) copy-start(bf16[4,8,100,128]{3,1,2,0:T(8,128)(2,1)S(1)} %all-to-all-done) | copy-start | bytes 2457604
  40.5 28.7 %all-to-all-start.1 = ((f16[16,49,512]{2,1,0:T(8,128)(2,1)}), f16[16,49,512]{2,1,0:T(8,128)(2,1)}, u32[]{:S(2)}, u32[]{:S(2)}) async-start(f16[16,49,512]{2,1,0:T(8,128)(2,1)} %concatenate.3), calls=%async_computation.1 | async-start | bytes 1835008 | tf_op jit(solution)/shard_map/all_to_all | solution.py:33

commit v2 on v1

v2 whole, which is shorter than its diff:
```python
import jax
import jax.numpy as jnp
from jax import lax
from jax.sharding import Mesh, PartitionSpec as P


def power_of_two_shift(values):
    return jnp.clip(14.0 - jnp.ceil(jnp.log2(jnp.max(jnp.abs(values)))), -100.0, 100.0)


def pack(values, shift):
    scaled = (values * jnp.exp2(shift)).astype(jnp.float16)
    pad = [(0, 0, 0)] * (values.ndim - 2) + [(0, 1, 0), (0, 0, 0)]
    return lax.pad(scaled, shift.astype(jnp.float16), pad)


def unpack(received):
    unscale = jnp.exp2(-received[..., -1:, :].astype(jnp.float32))
    return received[..., :-1, :].astype(jnp.float32) * unscale


def body(field, send_blocks, send_count, regrid_weights, tile_slot, edge_inputs, cotangent):
    sample = field[0]
    own_lists = send_blocks[0]
    shards = own_lists.shape[0]
    slots_each = own_lists.shape[1]
    groups = lax.axis_size("group")
    place = lax.axis_index("sp")

    def to_shift(k):
        return [(i, (i + k) % shards) for i in range(shards)]

    outgoing = []
    for k in range(shards):
        dest = (place + k) % shards
        alive = jnp.arange(slots_each, dtype=jnp.int32) < send_count[0, dest]
        outgoing.append(
            jnp.where(alive[:, None, None], sample[own_lists[dest]], jnp.zeros((), jnp.bfloat16))
        )
    edge_inputs, cotangent, *outgoing = lax.optimization_barrier((edge_inputs, cotangent, *outgoing))
    incoming = [outgoing[0]] + [
        lax.ppermute(outgoing[k], "sp", to_shift(k)) for k in range(1, shards)
    ]

    partial_grad = lax.dot_general(
        edge_inputs, cotangent, (((0,), (0,)), ((), ())), preferred_element_type=jnp.float32
    )
    rows = partial_grad.shape[0] // (groups * 2 * shards)
    hid = partial_grad.shape[1]
    halves = partial_grad.reshape(groups, 2, shards * rows, hid)
    first = lax.axis_index("pair") == 0
    keep = jnp.where(first, halves[:, 0], halves[:, 1])
    give = jnp.where(first, halves[:, 1], halves[:, 0])
    pair_sum = keep + lax.ppermute(give, "pair", [(0, 1), (1, 0)])
    received = lax.all_to_all(
        pack(pair_sum, power_of_two_shift(pair_sum)), "group", split_axis=0, concat_axis=0, tiled=True
    )
    rep_sum = jnp.sum(unpack(received), axis=0).reshape(shards, rows, hid)
    shift = power_of_two_shift(rep_sum)
    weight_grad = lax.dynamic_index_in_dim(rep_sum, place, 0, keepdims=False)
    for k in range(1, shards):
        chunk = lax.dynamic_index_in_dim(rep_sum, (place + k) % shards, 0, keepdims=False)
        weight_grad = weight_grad + unpack(lax.ppermute(pack(chunk, shift), "sp", to_shift(k)))

    block_pool = jnp.concatenate(incoming, axis=0)
    source = tile_slot // slots_each
    slot = (place - source) % shards * slots_each + tile_slot % slots_each
    hidden = jnp.einsum(
        "tbcx,tbxn->tcn", block_pool[slot], regrid_weights, preferred_element_type=jnp.float32
    )
    hidden = hidden.astype(jnp.bfloat16)[None]
    return (hidden, weight_grad)


def solution(mesh):
    split = Mesh(
        mesh.devices.reshape(mesh.shape["rep"] // 2, 2, mesh.shape["sp"]), ("group", "pair", "sp")
    )
    rep = ("group", "pair")
    in_specs = (
        P(rep, "sp", None, None),
        P("sp", None, None),
        P("sp", None),
        P("sp", None, None, None),
        P("sp", None),
        P((*rep, "sp"), None),
        P((*rep, "sp"), None),
    )
    out_specs = (P(rep, "sp", None, None), P((*rep, "sp"), None))
    return jax.shard_map(body, mesh=split, in_specs=in_specs, out_specs=out_specs, check_vma=False)
```

time: 72.5 us -> 80.5 us (1.11)
  waiting for transfers between devices: 30.7 us -> 21.8 us
  local copies, waits for them, and re-layouts: 8.11 us -> 16.3 us
  starting transfers between devices: 11.5 us -> 18.6 us
  other arithmetic: 14 us -> 17.6 us
  matrix products: 6.28 us -> 3.12 us
  between operations: 1.48 us -> 2.38 us
    all_to_all x2 -> x1, waiting for transfers between devices: 30.7 us -> 0.01 us  [body(): lax.all_to_all(pack(pair_sum, power_of_two_shift(pair_sum)), 'group', spl...]
    ppermute x0 -> x6, waiting for transfers between devices: none -> 18.7 us  [the longest x3 12.8 us: body(): lax.ppermute(outgoing[k], 'sp', to_shift(k))]
    ppermute x0 -> x6, starting transfers between devices: none -> 13 us  [the longest x3 6.92 us: body(): lax.ppermute(pack(chunk, shift), 'sp', to_shift(k))]
    gather x2 -> x5, local copies, waits for them, and re-layouts: 3.58 us -> 9.9 us  [the longest x4 7.91 us: body(): sample[own_lists[dest]]]
    all_to_all x2 -> x1, starting transfers between devices: 11 us -> 5.07 us  [body(): lax.all_to_all(pack(pair_sum, power_of_two_shift(pair_sum)), 'group', spl...]
    select_n x3 -> x6, other arithmetic: 2.2 us -> 6.08 us  [the longest x4 5.18 us: body(): jnp.where(alive[:, None, None], sample[own_lists[dest]], jnp.zeros((), jn...]
    dot_general x1, matrix products: 4.16 us -> 1.01 us  [body(): lax.dot_general(edge_inputs, cotangent, (((0,), (0,)), ((), ())), preferr...]
    select_n x1, other arithmetic: 3.5 us -> 0.34 us  [body(): give = jnp.where(first, halves[:, 1], halves[:, 0])]
  transfers between devices with their start and end apart: 3 -> 8, of which waited for: 2 -> 5; matrix products, arithmetic and copies ran while one was open for 25% -> 8% of each run, Pallas kernels for 0% -> 0%
where the time goes in v2:
time: 80.5 us; the launch traced here: 79.8 us
  waiting for transfers between devices  21.8 us (27%)
  starting transfers between devices  18.6 us (23%)
  other arithmetic  17.6 us (22%)
  local copies, waits for them, and re-layouts  16.3 us (20%)
  matrix products  3.12 us (4%)
  between operations  2.38 us (3%)
    ppermute x3, waiting for transfers between devices, body(): lax.ppermute(outgoing[k], 'sp', to_shift(k))  12.8 us
    gather x4, local copies, waits for them, and re-layouts, body(): sample[own_lists[dest]]  7.91 us
    ppermute x3, starting transfers between devices, body(): lax.ppermute(pack(chunk, shift), 'sp', to_shift(k))  6.92 us
    ppermute x3, starting transfers between devices, body(): lax.ppermute(outgoing[k], 'sp', to_shift(k))  6.06 us
    ppermute x3, waiting for transfers between devices, body(): lax.ppermute(pack(chunk, shift), 'sp', to_shift(k))  5.95 us
    select_n x4, other arithmetic, body(): jnp.where(alive[:, None, None], sample[own_lists[dest]], jnp.zeros((), jn...  5.18 us
    all_to_all x1, starting transfers between devices, body(): lax.all_to_all(pack(pair_sum, power_of_two_shift(pair_sum)), 'group', spl...  5.07 us
    unnamed x21, local copies, waits for them, and re-layouts  3.8 us
  transfers between devices with their start and end apart: 8, of which 5 were waited for; matrix products, arithmetic and copies ran while one was open for 8% of the time, Pallas kernels for 0%

profile of v2, /device:TPU:0, one launch (start us, length us, event | category | flops | bytes accessed | tf_op | source)
XLA Modules:
  0.0 79.8 jit_solution(16771626958568080200)
XLA Ops:
  0.7 0.9 %fusion.29 = (s32[8]{0:T(128)S(1)}, s32[8]{0:T(128)S(1)}, s32[8]{0:T(128)S(1)}, s32[8]{0:T(128)S(1)}) fusion(s32[1,4,8]{2,1,0:T(4,128)} %param.8, s32[]{:T(128)S(6)} %select_n.150, s32[]{:T(128)S(6)} %select_n.142, s32[]{:T(128)S(6)} %select_n.138, s32[]{:T(128)S(6)} %select_n.146), kind=kLoop, calls=%fused_computation.83 | loop fusion | flops 96 | bytes 272 | tf_op jit(solution)/shard_map/select_n | solution.py:38
  1.6 1.5 %constant_dynamic-slice_fusion.1 = (s32[1,1]{1,0:T(1,128)}, s32[1,1]{1,0:T(1,128)}, s32[1,1]{1,0:T(1,128)}, s32[1,1]{1,0:T(1,128)}) fusion(s32[1,4]{1,0:T(1,128)} %param.9, s32[]{:T(128)S(6)} %select_n.150, s32[]{:T(128)S(6)} %select_n.142, s32[]{:T(128)S(6)} %select_n.138, s32[]{:T(128)S(6)} %select_n.146), kind=kLoop, calls=%fused_computation.57 | loop fusion | bytes 48 | tf_op jit(solution)/shard_map/dynamic_slice | solution.py:36
  5.6 1.5 %copy.26 = bf16[1,32,100,128]{3,2,1,0:T(8,128)(2,1)S(1)} copy(bf16[1,32,100,128]{3,1,2,0:T(8,128)(2,1)} %param.7) | data formatting | bytes 1638400 | tf_op args[0]
  7.1 0.9 %copy-done.2 = bf16[1,32,100,128]{3,2,1,0:T(8,128)(2,1)} copy-done((bf16[1,32,100,128]{3,2,1,0:T(8,128)(2,1)}, bf16[1,32,100,128]{3,2,1,0:T(8,128)(2,1)S(1)}, u32[]{:S(2)}) %copy-start.2) | copy-done | bytes 819224
  8.6 2.5 %gather_fusion.2 = bf16[8,100,128]{2,1,0:T(8,128)(2,1)} fusion(bf16[32,100,128]{2,1,0:T(8,128)(2,1)} %bitcast.92, s32[1024]{0:T(1024)S(1)} %get-tuple-element.32), kind=kCustom, calls=%fused_computation.2 | custom fusion | bytes 409632 | tf_op jit(solution)/shard_map/gather | solution.py:38
  11.1 2.4 %gather_fusion.1 = bf16[8,100,128]{2,1,0:T(8,128)(2,1)} fusion(bf16[32,100,128]{2,1,0:T(8,128)(2,1)} %bitcast.93, s32[1024]{0:T(1024)S(1)} %get-tuple-element.33), kind=kCustom, calls=%fused_computation.1 | custom fusion | bytes 409632 | tf_op jit(solution)/shard_map/gather | solution.py:38
  13.5 2.4 %gather_fusion = bf16[8,100,128]{2,1,0:T(8,128)(2,1)} fusion(bf16[32,100,128]{2,1,0:T(8,128)(2,1)} %bitcast.94, s32[1024]{0:T(1024)S(1)} %get-tuple-element.34), kind=kCustom, calls=%fused_computation | custom fusion | bytes 409632 | tf_op jit(solution)/shard_map/gather | solution.py:38
  16.0 0.8 broadcast_select_fusion
  16.7 1.7 %broadcast_select_fusion.1 = bf16[8,100,128]{2,1,0:T(8,128)(2,1)} fusion(bf16[8,100,128]{2,1,0:T(8,128)(2,1)} %gather_fusion.2, pred[8]{0:T(512)(128)(4,1)S(1)} %iota_compare_fusion.1), kind=kLoop, calls=%fused_computation.19 | loop fusion | flops 102400 | bytes 409608 | tf_op jit(solution)/shard_map/jit(_where)/select_n | solution.py:38
  18.4 1.0 %broadcast_select_fusion.3 = bf16[8,100,128]{2,1,0:T(8,128)(2,1)S(1)} fusion(bf16[8,100,128]{2,1,0:T(8,128)(2,1)} %gather_fusion, pred[8]{0:T(512)(128)(4,1)S(1)} %iota_compare_fusion.3), kind=kLoop, calls=%fused_computation.21 | loop fusion | flops 102400 | bytes 409608 | tf_op jit(solution)/shard_map/jit(_where)/select_n | solution.py:38
  19.4 1.7 %broadcast_select_fusion.2 = bf16[8,100,128]{2,1,0:T(8,128)(2,1)} fusion(bf16[8,100,128]{2,1,0:T(8,128)(2,1)} %gather_fusion.1, pred[8]{0:T(512)(128)(4,1)S(1)} %iota_compare_fusion.2), kind=kLoop, calls=%fused_computation.20 | loop fusion | flops 102400 | bytes 409608 | tf_op jit(solution)/shard_map/jit(_where)/select_n | solution.py:38
  21.1 1.0 %fusion.35 = f32[1536,512]{1,0:T(8,128)S(1)} fusion(bf16[384,1536]{1,0:T(8,128)(2,1)S(1)} %copy-done.1, bf16[384,512]{1,0:T(8,128)(2,1)S(1)} %copy-done.3), kind=kOutput, calls=%fused_computation.92 | convolution fusion | flops 603979776 | bytes 4718592 | tf_op jit(solution)/shard_map/dot_general | solution.py:45
  23.1 3.0 %collective-permute-done.3 = f32[4,192,512]{2,1,0:T(8,128)S(1)} collective-permute-done((f32[4,192,512]{2,1,0:T(8,128)S(1)}, f32[4,192,512]{2,1,0:T(8,128)S(1)}, u32[]{:S(2)}, u32[]{:S(2)}) %collective-permute-start.3) | collective-permute-done | bytes 1572896 | tf_op jit(solution)/shard_map/ppermute | solution.py:54
  26.1 2.3 %abs_reduce_fusion = (f32[]{:T(128)}, f32[4,192,512]{2,1,0:T(8,128)}) fusion(f32[4,192,512]{2,1,0:T(8,128)S(1)} %collective-permute-done.3, f32[4,2,192,512]{3,2,1,0:T(8,128)S(1)} %bitcast.87, pred[]{:T(512)S(6)} %eq.14), kind=kLoop, calls=%fused_computation.10 | loop fusion | flops 1572863 | bytes 6291461 | tf_op jit(solution)/shard_map/reduce_max | solution.py:8
  29.2 1.6 %multiply_convert_fusion = f16[4,192,512]{2,1,0:T(8,128)(2,1)S(1)} fusion(f32[4,192,512]{2,1,0:T(8,128)} %get-tuple-element.19, f32[]{:T(128)S(6)} %exp2.44), kind=kLoop, calls=%fused_computation.9 | loop fusion | flops 786432 | bytes 2359300 | tf_op jit(solution)/shard_map/convert_element_type | solution.py:12
  30.8 1.1 %pad.12 = f16[4,193,512]{2,1,0:T(8,128)(2,1)} pad(f16[4,192,512]{2,1,0:T(8,128)(2,1)S(1)} %multiply_convert_fusion, f16[]{:T(256)S(6)} %convert_element_type.58), padding=0_0x0_1x0_0 | pad | bytes 1576962 | tf_op jit(solution)/shard_map/pad | solution.py:14
  31.9 5.1 %all-to-all-start = ((f16[4,193,512]{2,1,0:T(8,128)(2,1)}), f16[4,193,512]{2,1,0:T(8,128)(2,1)}, u32[]{:S(2)}, u32[]{:S(2)}) async-start(f16[4,193,512]{2,1,0:T(8,128)(2,1)} %pad.12), calls=%async_computation | async-start | bytes 1638400 | tf_op jit(solution)/shard_map/all_to_all | solution.py:55
  37.0 2.1 %collective-permute-start = (bf16[8,100,128]{2,1,0:T(8,128)(2,1)S(1)}, bf16[8,100,128]{2,1,0:T(8,128)(2,1)S(1)}, u32[]{:S(2)}, u32[]{:S(2)}) collective-permute-start(bf16[8,100,128]{2,1,0:T(8,128)(2,1)S(1)} %copy-done.6), channel_id=1, source_target_pairs={{0,1},{1,2},{2,3},{3,0},{4,5},{5,6},{6,7},{7,4},{8,9},{9,10},{10,1... | collective-permute-start | bytes 614408 | tf_op jit(solution)/shard_map/ppermute | solution.py:42
  39.1 2.6 %collective-permute-start.1 = (bf16[8,100,128]{2,1,0:T(8,128)(2,1)S(1)}, bf16[8,100,128]{2,1,0:T(8,128)(2,1)S(1)}, u32[]{:S(2)}, u32[]{:S(2)}) collective-permute-start(bf16[8,100,128]{2,1,0:T(8,128)(2,1)S(1)} %copy-done.5), channel_id=1, source_target_pairs={{0,2},{1,3},{2,0},{3,1},{4,6},{5,7},{6,4},{7,5},{8,10},{9,11},{10,... | collective-permute-start | bytes 614408 | tf_op jit(solution)/shard_map/ppermute | solution.py:42
  41.7 1.3 %collective-permute-start.2 = (bf16[8,100,128]{2,1,0:T(8,128)(2,1)S(1)}, bf16[8,100,128]{2,1,0:T(8,128)(2,1)}, u32[]{:S(2)}, u32[]{:S(2)}) collective-permute-start(bf16[8,100,128]{2,1,0:T(8,128)(2,1)S(1)} %copy-done.4), channel_id=1, source_target_pairs={{0,3},{1,0},{2,1},{3,2},{4,7},{5,4},{6,5},{7,6},{8,11},{9,8},{10,9... | collective-permute-start | bytes 614408 | tf_op jit(solution)/shard_map/ppermute | solution.py:42
  43.2 4.2 %collective-permute-done = bf16[8,100,128]{2,1,0:T(8,128)(2,1)S(1)} collective-permute-done((bf16[8,100,128]{2,1,0:T(8,128)(2,1)S(1)}, bf16[8,100,128]{2,1,0:T(8,128)(2,1)S(1)}, u32[]{:S(2)}, u32[]{:S(2)}) %collective-permute-start) | collective-permute-done | bytes 204832 | tf_op jit(solution)/shard_map/ppermute | solution.py:42
  47.4 8.6 %collective-permute-done.1 = bf16[8,100,128]{2,1,0:T(8,128)(2,1)S(1)} collective-permute-done((bf16[8,100,128]{2,1,0:T(8,128)(2,1)S(1)}, bf16[8,100,128]{2,1,0:T(8,128)(2,1)S(1)}, u32[]{:S(2)}, u32[]{:S(2)}) %collective-permute-start.1) | collective-permute-done | bytes 204832 | tf_op jit(solution)/shard_map/ppermute | solution.py:42
  56.6 1.1 %pad_maximum_fusion = bf16[32,100,128]{2,1,0:T(8,128)(2,1)S(1)} fusion(bf16[8,100,128]{2,1,0:T(8,128)(2,1)} %collective-permute-done.2, bf16[8,100,128]{2,1,0:T(8,128)(2,1)} %copy-done.7, bf16[8,100,128]{2,1,0:T(8,128)(2,1)S(1)} %collective-permute-done, bf16[8,100,128]{2,1,0:T(8,128)(2,1)S(1)} %broadcast_select_fusion.3), kind=kLoop, calls=%fused_computation.15 | loop fusion | flops 1228800 | bytes 1638400 | tf_op jit(solution)/shard_map/concatenate | solution.py:65
  57.8 2.0 %gather_fusion.4 = bf16[64,100,128]{2,1,0:T(8,128)(2,1)} fusion(bf16[32,100,128]{2,1,0:T(8,128)(2,1)S(1)} %pad_maximum_fusion, s32[1024]{0:T(1024)S(1)} %pad_clamp_fusion), kind=kCustom, calls=%fused_computation.4 | custom fusion | bytes 3277056 | tf_op jit(solution)/shard_map/gather | solution.py:69
  59.8 0.8 fusion.11
  60.6 1.3 %multiply_reduce_fusion = f32[192,512]{1,0:T(8,128)S(1)} fusion(f16[4,193,512]{2,1,0:T(8,128)(2,1)} %all-to-all-done, f32[4,512]{1,0:T(4,128)S(1)} %bitcast.95), kind=kLoop, calls=%fused_computation.8 | loop fusion | flops 1081344 | bytes 1187840 | tf_op jit(solution)/shard_map/reduce_sum | solution.py:58
  63.4 3.4 %collective-permute-start.5 = (f16[49,512]{1,0:T(8,128)(2,1)S(1)}, f16[49,512]{1,0:T(8,128)(2,1)S(1)}, u32[]{:S(2)}, u32[]{:S(2)}) collective-permute-start(f16[49,512]{1,0:T(8,128)(2,1)S(1)} %pad.14), channel_id=1, source_target_pairs={{0,2},{1,3},{2,0},{3,1},{4,6},{5,7},{6,4},{7,5},{8,10},{9,11},{10,... | collective-permute-start | bytes 150536 | tf_op jit(solution)/shard_map/ppermute | solution.py:63
  66.7 2.1 %fusion.3 = bf16[1,8,100,128]{3,2,1,0:T(8,128)(2,1)S(1)} fusion(bf16[8,8,100,128]{3,2,1,0:T(8,128)(2,1)} %bitcast.88, bf16[8,8,128,128]{3,2,1,0:T(8,128)(2,1)S(1)} %copy-done), kind=kOutput, calls=%fused_computation.14 | convolution fusion | flops 209817600 | bytes 3940352 | tf_op jit(solution)/shard_map/tbcx,tbxn->tcn/dot_general | solution.py:68
  68.9 0.7 copy.20
  69.6 3.5 %collective-permute-start.6 = (f16[49,512]{1,0:T(8,128)(2,1)S(1)}, f16[49,512]{1,0:T(8,128)(2,1)S(1)}, u32[]{:S(2)}, u32[]{:S(2)}) collective-permute-start(f16[49,512]{1,0:T(8,128)(2,1)S(1)} %pad.15), channel_id=1, source_target_pairs={{0,3},{1,0},{2,1},{3,2},{4,7},{5,4},{6,5},{7,6},{8,11},{9,8},{10,9... | collective-permute-start | bytes 150536 | tf_op jit(solution)/shard_map/ppermute | solution.py:63
  73.2 2.0 %collective-permute-done.6 = f16[49,512]{1,0:T(8,128)(2,1)S(1)} collective-permute-done((f16[49,512]{1,0:T(8,128)(2,1)S(1)}, f16[49,512]{1,0:T(8,128)(2,1)S(1)}, u32[]{:S(2)}, u32[]{:S(2)}) %collective-permute-start.6) | collective-permute-done | bytes 50208 | tf_op jit(solution)/shard_map/ppermute | solution.py:63
  75.1 4.0 %collective-permute-done.4 = f16[49,512]{1,0:T(8,128)(2,1)S(1)} collective-permute-done((f16[49,512]{1,0:T(8,128)(2,1)S(1)}, f16[49,512]{1,0:T(8,128)(2,1)S(1)}, u32[]{:S(2)}, u32[]{:S(2)}) %collective-permute-start.4) | collective-permute-done | bytes 50208 | tf_op jit(solution)/shard_map/ppermute | solution.py:63
  (43 shorter events, 6.4 us)
Async XLA Ops:
  0.6 66.1 %copy-start = (bf16[8,8,128,128]{3,2,1,0:T(8,128)(2,1)S(1)}, bf16[8,8,128,128]{3,2,1,0:T(8,128)(2,1)}, u32[]{:S(2)}) copy-start(bf16[8,8,128,128]{3,2,1,0:T(8,128)(2,1)} %param.10) | copy-start | bytes 6291460
  7.1 0.9 %copy-start.2 = (bf16[1,32,100,128]{3,2,1,0:T(8,128)(2,1)}, bf16[1,32,100,128]{3,2,1,0:T(8,128)(2,1)S(1)}, u32[]{:S(2)}) copy-start(bf16[1,32,100,128]{3,2,1,0:T(8,128)(2,1)S(1)} %copy.26) | copy-start | bytes 2457604
  8.6 12.5 %copy-start.1 = (bf16[384,1536]{1,0:T(8,128)(2,1)S(1)}, bf16[384,1536]{1,0:T(8,128)(2,1)}, u32[]{:S(2)}) copy-start(bf16[384,1536]{1,0:T(8,128)(2,1)} %param.12) | copy-start | bytes 3538948
  16.0 5.2 %copy-start.3 = (bf16[384,512]{1,0:T(8,128)(2,1)S(1)}, bf16[384,512]{1,0:T(8,128)(2,1)}, u32[]{:S(2)}) copy-start(bf16[384,512]{1,0:T(8,128)(2,1)} %param.13) | copy-start | bytes 1179652
  22.5 3.6 %collective-permute-start.3 = (f32[4,192,512]{2,1,0:T(8,128)S(1)}, f32[4,192,512]{2,1,0:T(8,128)S(1)}, u32[]{:S(2)}, u32[]{:S(2)}) collective-permute-start(f32[4,192,512]{2,1,0:T(8,128)S(1)} %select_bitcast_fusion), channel_id=1, source_target_pairs={{0,4},{4,0},{1,5},{5,1},{2,6},{6,2},{3,7},{7,3},{8,12},{12,8},{9,1... | collective-permute-start | bytes 4718600 | tf_op jit(solution)/shard_map/ppermute | solution.py:54
  30.8 6.2 %copy-start.6 = (bf16[8,100,128]{2,1,0:T(8,128)(2,1)S(1)}, bf16[8,100,128]{2,1,0:T(8,128)(2,1)}, u32[]{:S(2)}) copy-start(bf16[8,100,128]{2,1,0:T(8,128)(2,1)} %broadcast_select_fusion.2) | copy-start | bytes 614404
  30.8 8.3 %copy-start.5 = (bf16[8,100,128]{2,1,0:T(8,128)(2,1)S(1)}, bf16[8,100,128]{2,1,0:T(8,128)(2,1)}, u32[]{:S(2)}) copy-start(bf16[8,100,128]{2,1,0:T(8,128)(2,1)} %broadcast_select_fusion.1) | copy-start | bytes 614404
  30.8 10.9 %copy-start.4 = (bf16[8,100,128]{2,1,0:T(8,128)(2,1)S(1)}, bf16[8,100,128]{2,1,0:T(8,128)(2,1)}, u32[]{:S(2)}) copy-start(bf16[8,100,128]{2,1,0:T(8,128)(2,1)} %broadcast_select_fusion) | copy-start | bytes 614404
  30.8 12.2 %copy-start.8 = (s32[8,8]{1,0:T(8,128)S(1)}, s32[8,8]{1,0:T(8,128)}, u32[]{:S(2)}) copy-start(s32[8,8]{1,0:T(8,128)} %param.11) | copy-start | bytes 772
  31.9 27.9 %all-to-all-start = ((f16[4,193,512]{2,1,0:T(8,128)(2,1)}), f16[4,193,512]{2,1,0:T(8,128)(2,1)}, u32[]{:S(2)}, u32[]{:S(2)}) async-start(f16[4,193,512]{2,1,0:T(8,128)(2,1)} %pad.12), calls=%async_computation | async-start | bytes 1638400 | tf_op jit(solution)/shard_map/all_to_all | solution.py:55
  37.0 10.4 %collective-permute-start = (bf16[8,100,128]{2,1,0:T(8,128)(2,1)S(1)}, bf16[8,100,128]{2,1,0:T(8,128)(2,1)S(1)}, u32[]{:S(2)}, u32[]{:S(2)}) collective-permute-start(bf16[8,100,128]{2,1,0:T(8,128)(2,1)S(1)} %copy-done.6), channel_id=1, source_target_pairs={{0,1},{1,2},{2,3},{3,0},{4,5},{5,6},{6,7},{7,4},{8,9},{9,10},{10,1... | collective-permute-start | bytes 614408 | tf_op jit(solution)/shard_map/ppermute | solution.py:42
  39.1 16.8 %collective-permute-start.1 = (bf16[8,100,128]{2,1,0:T(8,128)(2,1)S(1)}, bf16[8,100,128]{2,1,0:T(8,128)(2,1)S(1)}, u32[]{:S(2)}, u32[]{:S(2)}) collective-permute-start(bf16[8,100,128]{2,1,0:T(8,128)(2,1)S(1)} %copy-done.5), channel_id=1, source_target_pairs={{0,2},{1,3},{2,0},{3,1},{4,6},{5,7},{6,4},{7,5},{8,10},{9,11},{10,... | collective-permute-start | bytes 614408 | tf_op jit(solution)/shard_map/ppermute | solution.py:42
  41.7 14.9 %collective-permute-start.2 = (bf16[8,100,128]{2,1,0:T(8,128)(2,1)S(1)}, bf16[8,100,128]{2,1,0:T(8,128)(2,1)}, u32[]{:S(2)}, u32[]{:S(2)}) collective-permute-start(bf16[8,100,128]{2,1,0:T(8,128)(2,1)S(1)} %copy-done.4), channel_id=1, source_target_pairs={{0,3},{1,0},{2,1},{3,2},{4,7},{5,4},{6,5},{7,6},{8,11},{9,8},{10,9... | collective-permute-start | bytes 614408 | tf_op jit(solution)/shard_map/ppermute | solution.py:42
  55.9 0.7 copy-start.7
  63.4 9.8 %collective-permute-start.5 = (f16[49,512]{1,0:T(8,128)(2,1)S(1)}, f16[49,512]{1,0:T(8,128)(2,1)S(1)}, u32[]{:S(2)}, u32[]{:S(2)}) collective-permute-start(f16[49,512]{1,0:T(8,128)(2,1)S(1)} %pad.14), channel_id=1, source_target_pairs={{0,2},{1,3},{2,0},{3,1},{4,6},{5,7},{6,4},{7,5},{8,10},{9,11},{10,... | collective-permute-start | bytes 150536 | tf_op jit(solution)/shard_map/ppermute | solution.py:63
  69.6 5.5 %collective-permute-start.6 = (f16[49,512]{1,0:T(8,128)(2,1)S(1)}, f16[49,512]{1,0:T(8,128)(2,1)S(1)}, u32[]{:S(2)}, u32[]{:S(2)}) collective-permute-start(f16[49,512]{1,0:T(8,128)(2,1)S(1)} %pad.15), channel_id=1, source_target_pairs={{0,3},{1,0},{2,1},{3,2},{4,7},{5,4},{6,5},{7,6},{8,11},{9,8},{10,9... | collective-permute-start | bytes 150536 | tf_op jit(solution)/shard_map/ppermute | solution.py:63
  73.1 6.0 %collective-permute-start.4 = (f16[49,512]{1,0:T(8,128)(2,1)S(1)}, f16[49,512]{1,0:T(8,128)(2,1)S(1)}, u32[]{:S(2)}, u32[]{:S(2)}) collective-permute-start(f16[49,512]{1,0:T(8,128)(2,1)S(1)} %pad.13), channel_id=1, source_target_pairs={{0,1},{1,2},{2,3},{3,0},{4,5},{5,6},{6,7},{7,4},{8,9},{9,10},{10,1... | collective-permute-start | bytes 150536 | tf_op jit(solution)/shard_map/ppermute | solution.py:63

commit v3 on v2

--- a/solution.py
+++ b/solution.py
@@ -10,8 +10,8 @@
 
 def pack(values, shift):
     scaled = (values * jnp.exp2(shift)).astype(jnp.float16)
-    pad = [(0, 0, 0)] * (values.ndim - 2) + [(0, 1, 0), (0, 0, 0)]
-    return lax.pad(scaled, shift.astype(jnp.float16), pad)
+    tag = jnp.broadcast_to(shift.astype(jnp.float16), values.shape[:-2] + (1, values.shape[-1]))
+    return jnp.concatenate([scaled, tag], axis=-2)
 
 
 def unpack(received):
@@ -19,7 +19,7 @@
     return received[..., :-1, :].astype(jnp.float32) * unscale
 
 
-def body(field, send_blocks, send_count, regrid_weights, tile_slot, edge_inputs, cotangent):
+def work(field, send_blocks, send_count, regrid_weights, tile_slot, edge_inputs, cotangent):
     sample = field[0]
     own_lists = send_blocks[0]
     shards = own_lists.shape[0]
@@ -30,21 +30,19 @@
     def to_shift(k):
         return [(i, (i + k) % shards) for i in range(shards)]
 
-    outgoing = []
-    for k in range(shards):
-        dest = (place + k) % shards
-        alive = jnp.arange(slots_each, dtype=jnp.int32) < send_count[0, dest]
-        outgoing.append(
-            jnp.where(alive[:, None, None], sample[own_lists[dest]], jnp.zeros((), jnp.bfloat16))
-        )
-    edge_inputs, cotangent, *outgoing = lax.optimization_barrier((edge_inputs, cotangent, *outgoing))
+    k_dest = (place + jnp.arange(shards, dtype=jnp.int32)) % shards
+    pick_dest = k_dest[:, None] == jnp.arange(shards, dtype=jnp.int32)[None, :]
+    alive = jnp.arange(slots_each, dtype=jnp.int32)[None, :] < send_count[0][:, None]
+    live_list = jnp.where(alive, own_lists, -1)
+    rolled = jnp.sum(jnp.where(pick_dest[:, :, None], live_list[None], 0), axis=1)
+    blocks = jnp.arange(sample.shape[0], dtype=jnp.int32)
+    choose = (rolled[:, :, None] == blocks).astype(jnp.bfloat16)
+    outgoing = jnp.einsum("kjb,bcx->kjcx", choose, sample, preferred_element_type=jnp.bfloat16)
     incoming = [outgoing[0]] + [
         lax.ppermute(outgoing[k], "sp", to_shift(k)) for k in range(1, shards)
     ]
 
-    partial_grad = lax.dot_general(
-        edge_inputs, cotangent, (((0,), (0,)), ((), ())), preferred_element_type=jnp.float32
-    )
+    partial_grad = lax.dot_general(edge_inputs, cotangent, (((0,), (0,)), ((), ())), preferred_element_type=jnp.float32)
     rows = partial_grad.shape[0] // (groups * 2 * shards)
     hid = partial_grad.shape[1]
     halves = partial_grad.reshape(groups, 2, shards * rows, hid)
@@ -56,7 +54,8 @@
         pack(pair_sum, power_of_two_shift(pair_sum)), "group", split_axis=0, concat_axis=0, tiled=True
     )
     rep_sum = jnp.sum(unpack(received), axis=0).reshape(shards, rows, hid)
-    shift = power_of_two_shift(rep_sum)
+    shift = jnp.min(received[:, -1, :].astype(jnp.float32), axis=0) - float((groups - 1).bit_length())
+    shift = shift[None, :]
     weight_grad = lax.dynamic_index_in_dim(rep_sum, place, 0, keepdims=False)
     for k in range(1, shards):
         chunk = lax.dynamic_index_in_dim(rep_sum, (place + k) % shards, 0, keepdims=False)
@@ -87,4 +86,4 @@
         P((*rep, "sp"), None),
     )
     out_specs = (P(rep, "sp", None, None), P((*rep, "sp"), None))
-    return jax.shard_map(body, mesh=split, in_specs=in_specs, out_specs=out_specs, check_vma=False)
+    return jax.shard_map(work, mesh=split, in_specs=in_specs, out_specs=out_specs, check_vma=False)

time: 80.5 us -> 60.1 us (0.75)
  local copies, waits for them, and re-layouts: 16.3 us -> 5.31 us
  other arithmetic: 17.6 us -> 11.5 us
  waiting for transfers between devices: 21.8 us -> 17.7 us
  matrix products: 3.12 us -> 4.74 us
  between operations: 2.38 us -> 1.55 us
    gather x5 -> x1, local copies, waits for them, and re-layouts: 9.9 us -> 2 us  [work(): block_pool[slot]]
    select_n x7 -> x3, other arithmetic: 6.43 us -> 1.81 us  [the longest x1 1.77 us: work(): give = jnp.where(first, halves[:, 1], halves[:, 0])]
    ppermute x7, waiting for transfers between devices: 21.8 us -> 17.7 us  [the longest x3 12.4 us: work(): lax.ppermute(outgoing[k], 'sp', to_shift(k))]
    unnamed x21 -> x14, local copies, waits for them, and re-layouts: 3.8 us -> 1.11 us
    lt x4 -> x0, other arithmetic: 2.57 us -> none  [body(): alive = jnp.arange(slots_each, dtype=jnp.int32) < send_count[0, dest]]
    reduce_max x2 -> x1, other arithmetic: 2.94 us -> 4.66 us  [power_of_two_shift(): jnp.max(jnp.abs(values))]
    dot_general x2 -> x3, matrix products: 3.12 us -> 4.74 us  [the longest x1 2.51 us: work(): lax.dot_general(edge_inputs, cotangent, (((0,), (0,)), ((), ())), preferr...]
    dynamic_slice x1 -> x0, local copies, waits for them, and re-layouts: 1.45 us -> none  [body(): alive = jnp.arange(slots_each, dtype=jnp.int32) < send_count[0, dest]]
  transfers between devices with their start and end apart: 8 -> 8, of which waited for: 5 -> 5; matrix products, arithmetic and copies ran while one was open for 8% -> 11% of each run, Pallas kernels for 0% -> 0%
where the time goes in v3:
time: 60.1 us; the launch traced here: 59.8 us
  starting transfers between devices  19 us (32%)
  waiting for transfers between devices  17.7 us (29%)
  other arithmetic  11.5 us (19%)
  local copies, waits for them, and re-layouts  5.31 us (9%)
  matrix products  4.74 us (8%)
  between operations  1.55 us (3%)
    ppermute x3, waiting for transfers between devices, work(): lax.ppermute(outgoing[k], 'sp', to_shift(k))  12.4 us
    ppermute x3, starting transfers between devices, work(): lax.ppermute(pack(chunk, shift), 'sp', to_shift(k))  7.29 us
    ppermute x3, starting transfers between devices, work(): lax.ppermute(outgoing[k], 'sp', to_shift(k))  6.01 us
    all_to_all x1, starting transfers between devices, work(): lax.all_to_all(pack(pair_sum, power_of_two_shift(pair_sum)), 'group', spl...  5.2 us
    reduce_max x1, other arithmetic, power_of_two_shift(): jnp.max(jnp.abs(values))  4.66 us
    ppermute x3, waiting for transfers between devices, work(): lax.ppermute(pack(chunk, shift), 'sp', to_shift(k))  3.67 us
    dot_general x1, matrix products, work(): lax.dot_general(edge_inputs, cotangent, (((0,), (0,)), ((), ())), preferr...  2.51 us
    gather x1, local copies, waits for them, and re-layouts, work(): block_pool[slot]  2 us
  transfers between devices with their start and end apart: 8, of which 5 were waited for; matrix products, arithmetic and copies ran while one was open for 11% of the time, Pallas kernels for 0%

profile of v3, /device:TPU:0, one launch (start us, length us, event | category | flops | bytes accessed | tf_op | source)
XLA Modules:
  0.0 59.8 jit_solution(528738921043547293)
XLA Ops:
  0.7 2.5 %fusion.31 = f32[1536,512]{1,0:T(8,128)S(1)} fusion(bf16[384,1536]{1,0:T(8,128)(2,1)} %param.12, bf16[384,512]{1,0:T(8,128)(2,1)} %param.13), kind=kOutput, calls=%fused_computation.75 | convolution fusion | flops 603979776 | bytes 4718592 | tf_op jit(solution)/shard_map/dot_general | solution.py:45
  3.2 1.8 %select_bitcast_fusion = f32[4,192,512]{2,1,0:T(8,128)} fusion(f32[4,2,192,512]{3,2,1,0:T(8,128)S(1)} %bitcast.81, pred[]{:T(512)S(6)} %eq.48), kind=kLoop, calls=%fused_computation.7 | loop fusion | flops 393216 | bytes 4718593 | tf_op jit(solution)/shard_map/jit(_where)/select_n | solution.py:51
  5.0 0.4 copy-done.1
  5.3 0.5 collective-permute-start.3
  5.8 0.1 iota_compare_fusion.2
  6.0 0.1 select_reduce_fusion
  6.1 1.6 %fusion.4 = bf16[4,8,100,128]{3,1,2,0:T(8,128)(2,1)S(1)} fusion(bf16[1,32,100,128]{3,1,2,0:T(8,128)(2,1)} %param.7, s32[4,8]{1,0:T(4,128)S(1)} %select_reduce_fusion), kind=kOutput, calls=%fused_computation.12 | convolution fusion | flops 26215424 | bytes 1638528 | tf_op jit(solution)/shard_map/kjb,bcx->kjcx/dot_general | solution.py:40
  7.6 1.6 %collective-permute-done.3 = f32[4,192,512]{2,1,0:T(8,128)} collective-permute-done((f32[4,192,512]{2,1,0:T(8,128)}, f32[4,192,512]{2,1,0:T(8,128)}, u32[]{:S(2)}, u32[]{:S(2)}) %collective-permute-start.3) | collective-permute-done | bytes 1572896 | tf_op jit(solution)/shard_map/ppermute | solution.py:52
  9.2 4.7 %abs_reduce_fusion = (f32[]{:T(128)}, f32[4,192,512]{2,1,0:T(8,128)}) fusion(f32[4,192,512]{2,1,0:T(8,128)} %collective-permute-done.3, f32[4,2,192,512]{3,2,1,0:T(8,128)} %bitcast.82, pred[]{:T(512)S(6)} %eq.48), kind=kLoop, calls=%fused_computation.6 | loop fusion | flops 1572863 | bytes 6291461 | tf_op jit(solution)/shard_map/reduce_max | solution.py:8
  14.6 1.6 %multiply_convert_fusion = f16[4,192,512]{2,1,0:T(8,128)(2,1)S(1)} fusion(f32[4,192,512]{2,1,0:T(8,128)} %get-tuple-element.9, f32[]{:T(128)S(6)} %exp2.54), kind=kLoop, calls=%fused_computation.5 | loop fusion | flops 786432 | bytes 2359300 | tf_op jit(solution)/shard_map/convert_element_type | solution.py:12
  16.2 1.1 %concatenate.16 = f16[4,193,512]{2,1,0:T(8,128)(2,1)} pad(f16[4,192,512]{2,1,0:T(8,128)(2,1)S(1)} %multiply_convert_fusion, f16[]{:T(256)S(6)} %convert_element_type.63), padding=0_0x0_1x0_0 | pad | bytes 1576962 | tf_op jit(solution)/shard_map/concatenate | solution.py:14
  17.3 5.2 %all-to-all-start = ((f16[4,193,512]{2,1,0:T(8,128)(2,1)}), f16[4,193,512]{2,1,0:T(8,128)(2,1)}, u32[]{:S(2)}, u32[]{:S(2)}) async-start(f16[4,193,512]{2,1,0:T(8,128)(2,1)} %concatenate.16), calls=%async_computation | async-start | bytes 1638400 | tf_op jit(solution)/shard_map/all_to_all | solution.py:53
  22.5 0.7 %slice_bitcast_fusion.3 = (bf16[8,100,128]{2,0,1:T(8,128)(2,1)S(1)}, bf16[8,100,128]{2,0,1:T(8,128)(2,1)S(1)}, bf16[8,100,128]{2,0,1:T(8,128)(2,1)S(1)}, bf16[8,100,128]{2,0,1:T(8,128)(2,1)}) fusion(bf16[4,8,100,128]{3,1,2,0:T(8,128)(2,1)S(1)} %fusion.4), kind=kLoop, calls=%fused_computation.17 | loop fusion | bytes 1638400 | tf_op jit(solution)/shard_map/squeeze | solution.py:41
  23.2 2.1 %collective-permute-start = (bf16[8,100,128]{2,0,1:T(8,128)(2,1)}, bf16[8,100,128]{2,0,1:T(8,128)(2,1)S(1)}, u32[]{:S(2)}, u32[]{:S(2)}) collective-permute-start(bf16[8,100,128]{2,0,1:T(8,128)(2,1)} %get-tuple-element.15), channel_id=1, source_target_pairs={{0,1},{1,2},{2,3},{3,0},{4,5},{5,6},{6,7},{7,4},{8,9},{9,10},{10,1... | collective-permute-start | bytes 614408 | tf_op jit(solution)/shard_map/ppermute | solution.py:42
  25.3 2.6 %collective-permute-start.1 = (bf16[8,100,128]{2,0,1:T(8,128)(2,1)S(1)}, bf16[8,100,128]{2,0,1:T(8,128)(2,1)S(1)}, u32[]{:S(2)}, u32[]{:S(2)}) collective-permute-start(bf16[8,100,128]{2,0,1:T(8,128)(2,1)S(1)} %get-tuple-element.14), channel_id=1, source_target_pairs={{0,2},{1,3},{2,0},{3,1},{4,6},{5,7},{6,4},{7,5},{8,10},{9,11},{10,... | collective-permute-start | bytes 614408 | tf_op jit(solution)/shard_map/ppermute | solution.py:42
  27.9 1.3 %collective-permute-start.2 = (bf16[8,100,128]{2,0,1:T(8,128)(2,1)S(1)}, bf16[8,100,128]{2,0,1:T(8,128)(2,1)S(1)}, u32[]{:S(2)}, u32[]{:S(2)}) collective-permute-start(bf16[8,100,128]{2,0,1:T(8,128)(2,1)S(1)} %get-tuple-element.13), channel_id=1, source_target_pairs={{0,3},{1,0},{2,1},{3,2},{4,7},{5,4},{6,5},{7,6},{8,11},{9,8},{10,9... | collective-permute-start | bytes 614408 | tf_op jit(solution)/shard_map/ppermute | solution.py:42
  29.3 0.1 reshape.110
  29.4 4.2 %collective-permute-done = bf16[8,100,128]{2,0,1:T(8,128)(2,1)S(1)} collective-permute-done((bf16[8,100,128]{2,0,1:T(8,128)(2,1)}, bf16[8,100,128]{2,0,1:T(8,128)(2,1)S(1)}, u32[]{:S(2)}, u32[]{:S(2)}) %collective-permute-start) | collective-permute-done | bytes 204832 | tf_op jit(solution)/shard_map/ppermute | solution.py:42
  33.6 8.2 %collective-permute-done.1 = bf16[8,100,128]{2,0,1:T(8,128)(2,1)S(1)} collective-permute-done((bf16[8,100,128]{2,0,1:T(8,128)(2,1)S(1)}, bf16[8,100,128]{2,0,1:T(8,128)(2,1)S(1)}, u32[]{:S(2)}, u32[]{:S(2)}) %collective-permute-start.1) | collective-permute-done | bytes 204832 | tf_op jit(solution)/shard_map/ppermute | solution.py:42
  41.8 0.1 pad_maximum_fusion
  42.0 0.3 copy.21
  42.3 2.0 %gather_fusion = bf16[64,100,128]{2,1,0:T(8,128)(2,1)} fusion(bf16[32,100,128]{2,1,0:T(8,128)(2,1)S(1)} %copy.21, s32[1024]{0:T(1024)S(1)} %pad_clamp_fusion), kind=kCustom, calls=%fused_computation | custom fusion | bytes 3277056 | tf_op jit(solution)/shard_map/gather | solution.py:68
  44.3 0.9 %fusion.14 = (f32[512]{0:T(512)S(1)}, f32[4,1,512]{2,1,0:T(1,128)S(1)}) fusion(f16[4,193,512]{2,1,0:T(8,128)(2,1)} %all-to-all-done), kind=kLoop, calls=%fused_computation.46 | loop fusion | flops 7680 | bytes 14336 | tf_op jit(solution)/shard_map/reduce_min | solution.py:57
  45.3 1.3 %multiply_reduce_fusion = f32[192,512]{1,0:T(8,128)S(1)} fusion(f16[4,193,512]{2,1,0:T(8,128)(2,1)} %all-to-all-done, f32[4,512]{1,0:T(4,128)S(1)} %bitcast.86), kind=kLoop, calls=%fused_computation.4 | loop fusion | flops 1081344 | bytes 1187840 | tf_op jit(solution)/shard_map/reduce_sum | solution.py:56
  46.7 4.9 %collective-permute-start.4 = (f16[49,512]{1,0:T(8,128)(2,1)S(1)}, f16[49,512]{1,0:T(8,128)(2,1)S(1)}, u32[]{:S(2)}, u32[]{:S(2)}) collective-permute-start(f16[49,512]{1,0:T(8,128)(2,1)S(1)} %get-tuple-element.19), channel_id=1, source_target_pairs={{0,1},{1,2},{2,3},{3,0},{4,5},{5,6},{6,7},{7,4},{8,9},{9,10},{10,1... | collective-permute-start | bytes 150536 | tf_op jit(solution)/shard_map/ppermute | solution.py:62
  51.6 0.7 %fusion.3 = bf16[1,8,100,128]{3,2,1,0:T(8,128)(2,1)S(1)} fusion(bf16[8,8,100,128]{3,2,1,0:T(8,128)(2,1)S(1)} %bitcast.83, bf16[8,8,128,128]{3,2,1,0:T(8,128)(2,1)S(1)} %copy-done), kind=kOutput, calls=%fused_computation.10 | convolution fusion | flops 209817600 | bytes 3940352 | tf_op jit(solution)/shard_map/tbcx,tbxn->tcn/dot_general | solution.py:67
  52.3 0.7 %copy.26 = bf16[1,8,100,128]{3,1,2,0:T(8,128)(2,1)} copy(bf16[1,8,100,128]{3,2,1,0:T(8,128)(2,1)S(1)} %fusion.3) | data formatting | bytes 409600
  53.0 1.6 %collective-permute-start.5 = (f16[49,512]{1,0:T(8,128)(2,1)S(1)}, f16[49,512]{1,0:T(8,128)(2,1)S(1)}, u32[]{:S(2)}, u32[]{:S(2)}) collective-permute-start(f16[49,512]{1,0:T(8,128)(2,1)S(1)} %get-tuple-element.20), channel_id=1, source_target_pairs={{0,2},{1,3},{2,0},{3,1},{4,6},{5,7},{6,4},{7,5},{8,10},{9,11},{10,... | collective-permute-start | bytes 150536 | tf_op jit(solution)/shard_map/ppermute | solution.py:62
  54.6 0.8 %collective-permute-start.6 = (f16[49,512]{1,0:T(8,128)(2,1)S(1)}, f16[49,512]{1,0:T(8,128)(2,1)S(1)}, u32[]{:S(2)}, u32[]{:S(2)}) collective-permute-start(f16[49,512]{1,0:T(8,128)(2,1)S(1)} %get-tuple-element.21), channel_id=1, source_target_pairs={{0,3},{1,0},{2,1},{3,2},{4,7},{5,4},{6,5},{7,6},{8,11},{9,8},{10,9... | collective-permute-start | bytes 150536 | tf_op jit(solution)/shard_map/ppermute | solution.py:62
  55.4 3.4 %collective-permute-done.5 = f16[49,512]{1,0:T(8,128)(2,1)S(1)} collective-permute-done((f16[49,512]{1,0:T(8,128)(2,1)S(1)}, f16[49,512]{1,0:T(8,128)(2,1)S(1)}, u32[]{:S(2)}, u32[]{:S(2)}) %collective-permute-start.5) | collective-permute-done | bytes 50208 | tf_op jit(solution)/shard_map/ppermute | solution.py:62
  58.8 0.3 collective-permute-done.6
  59.1 0.7 %fusion.10 = f32[48,512]{1,0:T(8,128)} fusion(f32[4,48,512]{2,1,0:T(8,128)S(1)} %bitcast.85, s32[]{:T(128)S(6)} %select_n.95, f16[49,512]{1,0:T(8,128)(2,1)S(1)} %collective-permute-done.6, f16[49,512]{1,0:T(8,128)(2,1)S(1)} %collective-permute-done.5, f16[49,512]{1,0:T(8,128)(2,1)S(1)} %collective-permute-done.4, f32[512]{0:T(512)S(1)} %bitcast.89, ...), kind=kLoop, calls=%fused_computation.29 | loop fusion | flops 221184 | bytes 350212 | tf_op jit(solution)/shard_map/add | solution.py:62
  (26 shorter events, 0.3 us)
Async XLA Ops:
  0.6 51.0 %copy-start = (bf16[8,8,128,128]{3,2,1,0:T(8,128)(2,1)S(1)}, bf16[8,8,128,128]{3,2,1,0:T(8,128)(2,1)}, u32[]{:S(2)}) copy-start(bf16[8,8,128,128]{3,2,1,0:T(8,128)(2,1)} %param.10) | copy-start | bytes 6291460
  3.2 2.2 %copy-start.1 = (f32[1536,512]{1,0:T(8,128)}, f32[1536,512]{1,0:T(8,128)S(1)}, u32[]{:S(2)}) copy-start(f32[1536,512]{1,0:T(8,128)S(1)} %fusion.31) | copy-start | bytes 9437188
  3.2 2.7 %copy-start.4 = (s32[1,4,8]{2,1,0:T(4,128)S(1)}, s32[1,4,8]{2,1,0:T(4,128)}, u32[]{:S(2)}) copy-start(s32[1,4,8]{2,1,0:T(4,128)} %param.8) | copy-start | bytes 388
  3.2 2.7 %copy-start.5 = (s32[1,4]{1,0:T(1,128)S(1)}, s32[1,4]{1,0:T(1,128)}, u32[]{:S(2)}) copy-start(s32[1,4]{1,0:T(1,128)} %param.9) | copy-start | bytes 52
  5.3 3.9 %collective-permute-start.3 = (f32[4,192,512]{2,1,0:T(8,128)}, f32[4,192,512]{2,1,0:T(8,128)}, u32[]{:S(2)}, u32[]{:S(2)}) collective-permute-start(f32[4,192,512]{2,1,0:T(8,128)} %select_bitcast_fusion), channel_id=1, source_target_pairs={{0,4},{4,0},{1,5},{5,1},{2,6},{6,2},{3,7},{7,3},{8,12},{12,8},{9,1... | collective-permute-start | bytes 4718600 | tf_op jit(solution)/shard_map/ppermute | solution.py:52
  17.3 12.0 %copy-start.3 = (s32[8,8]{1,0:T(8,128)S(1)}, s32[8,8]{1,0:T(8,128)}, u32[]{:S(2)}) copy-start(s32[8,8]{1,0:T(8,128)} %param.11) | copy-start | bytes 772
  17.3 27.0 %all-to-all-start = ((f16[4,193,512]{2,1,0:T(8,128)(2,1)}), f16[4,193,512]{2,1,0:T(8,128)(2,1)}, u32[]{:S(2)}, u32[]{:S(2)}) async-start(f16[4,193,512]{2,1,0:T(8,128)(2,1)} %concatenate.16), calls=%async_computation | async-start | bytes 1638400 | tf_op jit(solution)/shard_map/all_to_all | solution.py:53
  23.2 10.4 %collective-permute-start = (bf16[8,100,128]{2,0,1:T(8,128)(2,1)}, bf16[8,100,128]{2,0,1:T(8,128)(2,1)S(1)}, u32[]{:S(2)}, u32[]{:S(2)}) collective-permute-start(bf16[8,100,128]{2,0,1:T(8,128)(2,1)} %get-tuple-element.15), channel_id=1, source_target_pairs={{0,1},{1,2},{2,3},{3,0},{4,5},{5,6},{6,7},{7,4},{8,9},{9,10},{10,1... | collective-permute-start | bytes 614408 | tf_op jit(solution)/shard_map/ppermute | solution.py:42
  25.3 16.5 %collective-permute-start.1 = (bf16[8,100,128]{2,0,1:T(8,128)(2,1)S(1)}, bf16[8,100,128]{2,0,1:T(8,128)(2,1)S(1)}, u32[]{:S(2)}, u32[]{:S(2)}) collective-permute-start(bf16[8,100,128]{2,0,1:T(8,128)(2,1)S(1)} %get-tuple-element.14), channel_id=1, source_target_pairs={{0,2},{1,3},{2,0},{3,1},{4,6},{5,7},{6,4},{7,5},{8,10},{9,11},{10,... | collective-permute-start | bytes 614408 | tf_op jit(solution)/shard_map/ppermute | solution.py:42
  27.9 13.9 %collective-permute-start.2 = (bf16[8,100,128]{2,0,1:T(8,128)(2,1)S(1)}, bf16[8,100,128]{2,0,1:T(8,128)(2,1)S(1)}, u32[]{:S(2)}, u32[]{:S(2)}) collective-permute-start(bf16[8,100,128]{2,0,1:T(8,128)(2,1)S(1)} %get-tuple-element.13), channel_id=1, source_target_pairs={{0,3},{1,0},{2,1},{3,2},{4,7},{5,4},{6,5},{7,6},{8,11},{9,8},{10,9... | collective-permute-start | bytes 614408 | tf_op jit(solution)/shard_map/ppermute | solution.py:42
  44.3 7.3 %copy-start.2 = (bf16[64,100,128]{2,1,0:T(8,128)(2,1)S(1)}, bf16[64,100,128]{2,1,0:T(8,128)(2,1)}, u32[]{:S(2)}) copy-start(bf16[64,100,128]{2,1,0:T(8,128)(2,1)} %gather_fusion) | copy-start | bytes 4915204
  46.7 8.7 %collective-permute-start.4 = (f16[49,512]{1,0:T(8,128)(2,1)S(1)}, f16[49,512]{1,0:T(8,128)(2,1)S(1)}, u32[]{:S(2)}, u32[]{:S(2)}) collective-permute-start(f16[49,512]{1,0:T(8,128)(2,1)S(1)} %get-tuple-element.19), channel_id=1, source_target_pairs={{0,1},{1,2},{2,3},{3,0},{4,5},{5,6},{6,7},{7,4},{8,9},{9,10},{10,1... | collective-permute-start | bytes 150536 | tf_op jit(solution)/shard_map/ppermute | solution.py:62
  53.0 5.8 %collective-permute-start.5 = (f16[49,512]{1,0:T(8,128)(2,1)S(1)}, f16[49,512]{1,0:T(8,128)(2,1)S(1)}, u32[]{:S(2)}, u32[]{:S(2)}) collective-permute-start(f16[49,512]{1,0:T(8,128)(2,1)S(1)} %get-tuple-element.20), channel_id=1, source_target_pairs={{0,2},{1,3},{2,0},{3,1},{4,6},{5,7},{6,4},{7,5},{8,10},{9,11},{10,... | collective-permute-start | bytes 150536 | tf_op jit(solution)/shard_map/ppermute | solution.py:62
  54.6 4.5 %collective-permute-start.6 = (f16[49,512]{1,0:T(8,128)(2,1)S(1)}, f16[49,512]{1,0:T(8,128)(2,1)S(1)}, u32[]{:S(2)}, u32[]{:S(2)}) collective-permute-start(f16[49,512]{1,0:T(8,128)(2,1)S(1)} %get-tuple-element.21), channel_id=1, source_target_pairs={{0,3},{1,0},{2,1},{3,2},{4,7},{5,4},{6,5},{7,6},{8,11},{9,8},{10,9... | collective-permute-start | bytes 150536 | tf_op jit(solution)/shard_map/ppermute | solution.py:62

commit v4 on v3

--- a/solution.py
+++ b/solution.py
@@ -4,8 +4,8 @@
 from jax.sharding import Mesh, PartitionSpec as P
 
 
-def power_of_two_shift(values):
-    return jnp.clip(14.0 - jnp.ceil(jnp.log2(jnp.max(jnp.abs(values)))), -100.0, 100.0)
+def power_of_two_shift(bound):
+    return jnp.clip(14.0 - jnp.ceil(jnp.log2(bound)), -100.0, 100.0)
 
 
 def pack(values, shift):
@@ -42,17 +42,22 @@
         lax.ppermute(outgoing[k], "sp", to_shift(k)) for k in range(1, shards)
     ]
 
-    partial_grad = lax.dot_general(edge_inputs, cotangent, (((0,), (0,)), ((), ())), preferred_element_type=jnp.float32)
+    partial_grad = lax.dot_general(
+        edge_inputs, cotangent, (((0,), (0,)), ((), ())), preferred_element_type=jnp.float32
+    )
     rows = partial_grad.shape[0] // (groups * 2 * shards)
     hid = partial_grad.shape[1]
     halves = partial_grad.reshape(groups, 2, shards * rows, hid)
     first = lax.axis_index("pair") == 0
     keep = jnp.where(first, halves[:, 0], halves[:, 1])
     give = jnp.where(first, halves[:, 1], halves[:, 0])
-    pair_sum = keep + lax.ppermute(give, "pair", [(0, 1), (1, 0)])
-    received = lax.all_to_all(
-        pack(pair_sum, power_of_two_shift(pair_sum)), "group", split_axis=0, concat_axis=0, tiled=True
-    )
+    keep, give = lax.optimization_barrier((keep, give))
+    swap = [(0, 1), (1, 0)]
+    taken = lax.ppermute(give, "pair", swap)
+    own_max = jnp.max(jnp.maximum(jnp.abs(keep), jnp.abs(give)), axis=(0, 1))[None, :]
+    bound = own_max + lax.ppermute(own_max, "pair", swap)
+    packed = pack(keep + taken, power_of_two_shift(bound)[None])
+    received = lax.all_to_all(packed, "group", split_axis=0, concat_axis=0, tiled=True)
     rep_sum = jnp.sum(unpack(received), axis=0).reshape(shards, rows, hid)
     shift = jnp.min(received[:, -1, :].astype(jnp.float32), axis=0) - float((groups - 1).bit_length())
     shift = shift[None, :]

time: 60.1 us -> 55.2 us (0.918)
  waiting for transfers between devices: 17.7 us -> 16 us
  other arithmetic: 11.5 us -> 10 us
  local copies, waits for them, and re-layouts: 5.31 us -> 3.9 us
  between operations: 1.55 us -> 0.84 us
    reduce_max x1, other arithmetic: 4.66 us -> 1.56 us  [work(): jnp.max(jnp.maximum(jnp.abs(keep), jnp.abs(give)), axis=(0, 1))[None, :]]
    ppermute x1 -> x2, waiting for transfers between devices: 1.56 us -> 0.01 us  [the longest x1 0.01 us: work(): bound = own_max + lax.ppermute(own_max, 'pair', swap)]
    concatenate x1 -> x2, other arithmetic: 0.04 us -> 1.15 us  [pack(): return jnp.concatenate([scaled, tag], axis=-2)]
    concatenate x1 -> x0, local copies, waits for them, and re-layouts: 1.06 us -> none  [pack(): return jnp.concatenate([scaled, tag], axis=-2)]
  transfers between devices with their start and end apart: 8 -> 9, of which waited for: 5 -> 4; matrix products, arithmetic and copies ran while one was open for 11% -> 15% of each run, Pallas kernels for 0% -> 0%
where the time goes in v4:
time: 55.2 us; the launch traced here: 54.9 us
  starting transfers between devices  19.2 us (35%)
  waiting for transfers between devices  16 us (29%)
  other arithmetic  10 us (18%)
  matrix products  4.89 us (9%)
  local copies, waits for them, and re-layouts  3.9 us (7%)
  between operations  0.84 us (2%)
    ppermute x3, waiting for transfers between devices, work(): lax.ppermute(outgoing[k], 'sp', to_shift(k))  12.3 us
    ppermute x3, starting transfers between devices, work(): lax.ppermute(pack(chunk, shift), 'sp', to_shift(k))  7.29 us
    ppermute x3, starting transfers between devices, work(): lax.ppermute(outgoing[k], 'sp', to_shift(k))  6.02 us
    all_to_all x1, starting transfers between devices, work(): lax.all_to_all(packed, 'group', split_axis=0, concat_axis=0, tiled=True)  5.29 us
    ppermute x3, waiting for transfers between devices, work(): lax.ppermute(pack(chunk, shift), 'sp', to_shift(k))  3.67 us
    dot_general x1, matrix products, work(): lax.dot_general(edge_inputs, cotangent, (((0,), (0,)), ((), ())), preferr...  2.51 us
    gather x1, local copies, waits for them, and re-layouts, work(): block_pool[slot]  2 us
    convert_element_type x2, other arithmetic, pack(): scaled = (values * jnp.exp2(shift)).astype(jnp.float16)  1.86 us
  transfers between devices with their start and end apart: 9, of which 4 were waited for; matrix products, arithmetic and copies ran while one was open for 15% of the time, Pallas kernels for 0%

profile of v4, /device:TPU:0, one launch (start us, length us, event | category | flops | bytes accessed | tf_op | source)
XLA Modules:
  0.0 54.9 jit_solution(5851702114554271217)
XLA Ops:
  0.7 2.5 %fusion.29 = f32[1536,512]{1,0:T(8,128)S(1)} fusion(bf16[384,1536]{1,0:T(8,128)(2,1)} %param.12, bf16[384,512]{1,0:T(8,128)(2,1)} %param.13), kind=kOutput, calls=%fused_computation.78 | convolution fusion | flops 603979776 | bytes 4718592 | tf_op jit(solution)/shard_map/dot_general | solution.py:45
  3.2 0.4 fusion
  3.6 1.7 %select_bitcast_fusion = f32[4,192,512]{2,1,0:T(8,128)} fusion(f32[4,2,192,512]{3,2,1,0:T(8,128)S(1)} %bitcast.77, pred[]{:T(512)S(6)} %eq.48), kind=kLoop, calls=%fused_computation.6 | loop fusion | flops 393216 | bytes 4718593 | tf_op jit(solution)/shard_map/jit(_where)/select_n | solution.py:53
  5.2 0.5 collective-permute-start.3
  5.7 1.6 %maximum_reduce_fusion = f32[512]{0:T(512)S(1)} fusion(f32[4,192,512]{2,1,0:T(8,128)} %select_bitcast_fusion, f32[4,192,512]{2,1,0:T(8,128)S(1)} %fusion), kind=kLoop, calls=%fused_computation.5 | loop fusion | flops 1572352 | bytes 3147776 | tf_op jit(solution)/shard_map/reduce_max | solution.py:57
  7.3 0.1 collective-permute-start.4
  7.4 0.1 iota_compare_fusion.2
  7.5 0.1 select_reduce_fusion
  7.6 1.7 %fusion.3 = bf16[4,8,100,128]{3,1,2,0:T(8,128)(2,1)S(1)} fusion(bf16[1,32,100,128]{3,1,2,0:T(8,128)(2,1)} %param.7, s32[4,8]{1,0:T(4,128)S(1)} %select_reduce_fusion), kind=kOutput, calls=%fused_computation.12 | convolution fusion | flops 26215424 | bytes 1638528 | tf_op jit(solution)/shard_map/kjb,bcx->kjcx/dot_general | solution.py:40
  9.4 1.8 %multiply_convert_fusion = f16[4,192,512]{2,1,0:T(8,128)(2,1)S(1)} fusion(f32[4,192,512]{2,1,0:T(8,128)S(1)} %copy-done.2, f32[4,192,512]{2,1,0:T(8,128)} %collective-permute-done.3, f32[512]{0:T(512)S(1)} %bitcast.82), kind=kLoop, calls=%fused_computation.4 | loop fusion | flops 1179648 | bytes 3934208 | tf_op jit(solution)/shard_map/convert_element_type | solution.py:12
  11.2 1.1 %pad_maximum_fusion.1 = f16[4,193,512]{2,1,0:T(8,128)(2,1)} fusion(f16[4,1,512]{2,1,0:T(2,128)(2,1)S(1)} %broadcast_in_dim.57, f16[4,192,512]{2,1,0:T(8,128)(2,1)S(1)} %multiply_convert_fusion), kind=kLoop, calls=%fused_computation.11 | loop fusion | flops 395264 | bytes 1581056 | tf_op jit(solution)/shard_map/concatenate | solution.py:14
  12.4 5.3 %all-to-all-start = ((f16[4,193,512]{2,1,0:T(8,128)(2,1)}), f16[4,193,512]{2,1,0:T(8,128)(2,1)}, u32[]{:S(2)}, u32[]{:S(2)}) async-start(f16[4,193,512]{2,1,0:T(8,128)(2,1)} %pad_maximum_fusion.1), calls=%async_computation | async-start | bytes 1638400 | tf_op jit(solution)/shard_map/all_to_all | solution.py:60
  17.6 0.7 %slice_bitcast_fusion.3 = (bf16[8,100,128]{2,0,1:T(8,128)(2,1)S(1)}, bf16[8,100,128]{2,0,1:T(8,128)(2,1)S(1)}, bf16[8,100,128]{2,0,1:T(8,128)(2,1)S(1)}, bf16[8,100,128]{2,0,1:T(8,128)(2,1)}) fusion(bf16[4,8,100,128]{3,1,2,0:T(8,128)(2,1)S(1)} %fusion.3), kind=kLoop, calls=%fused_computation.17 | loop fusion | bytes 1638400 | tf_op jit(solution)/shard_map/squeeze | solution.py:41
  18.4 2.1 %collective-permute-start = (bf16[8,100,128]{2,0,1:T(8,128)(2,1)}, bf16[8,100,128]{2,0,1:T(8,128)(2,1)S(1)}, u32[]{:S(2)}, u32[]{:S(2)}) collective-permute-start(bf16[8,100,128]{2,0,1:T(8,128)(2,1)} %get-tuple-element.19), channel_id=1, source_target_pairs={{0,1},{1,2},{2,3},{3,0},{4,5},{5,6},{6,7},{7,4},{8,9},{9,10},{10,1... | collective-permute-start | bytes 614408 | tf_op jit(solution)/shard_map/ppermute | solution.py:42
  20.5 2.6 %collective-permute-start.1 = (bf16[8,100,128]{2,0,1:T(8,128)(2,1)S(1)}, bf16[8,100,128]{2,0,1:T(8,128)(2,1)S(1)}, u32[]{:S(2)}, u32[]{:S(2)}) collective-permute-start(bf16[8,100,128]{2,0,1:T(8,128)(2,1)S(1)} %get-tuple-element.18), channel_id=1, source_target_pairs={{0,2},{1,3},{2,0},{3,1},{4,6},{5,7},{6,4},{7,5},{8,10},{9,11},{10,... | collective-permute-start | bytes 614408 | tf_op jit(solution)/shard_map/ppermute | solution.py:42
  23.1 1.3 %collective-permute-start.2 = (bf16[8,100,128]{2,0,1:T(8,128)(2,1)S(1)}, bf16[8,100,128]{2,0,1:T(8,128)(2,1)S(1)}, u32[]{:S(2)}, u32[]{:S(2)}) collective-permute-start(bf16[8,100,128]{2,0,1:T(8,128)(2,1)S(1)} %get-tuple-element.17), channel_id=1, source_target_pairs={{0,3},{1,0},{2,1},{3,2},{4,7},{5,4},{6,5},{7,6},{8,11},{9,8},{10,9... | collective-permute-start | bytes 614408 | tf_op jit(solution)/shard_map/ppermute | solution.py:42
  24.5 0.1 reshape.132
  24.6 4.2 %collective-permute-done = bf16[8,100,128]{2,0,1:T(8,128)(2,1)S(1)} collective-permute-done((bf16[8,100,128]{2,0,1:T(8,128)(2,1)}, bf16[8,100,128]{2,0,1:T(8,128)(2,1)S(1)}, u32[]{:S(2)}, u32[]{:S(2)}) %collective-permute-start) | collective-permute-done | bytes 204832 | tf_op jit(solution)/shard_map/ppermute | solution.py:42
  28.8 8.1 %collective-permute-done.1 = bf16[8,100,128]{2,0,1:T(8,128)(2,1)S(1)} collective-permute-done((bf16[8,100,128]{2,0,1:T(8,128)(2,1)S(1)}, bf16[8,100,128]{2,0,1:T(8,128)(2,1)S(1)}, u32[]{:S(2)}, u32[]{:S(2)}) %collective-permute-start.1) | collective-permute-done | bytes 204832 | tf_op jit(solution)/shard_map/ppermute | solution.py:42
  36.9 0.1 pad_maximum_fusion
  37.0 0.3 copy.21
  37.4 2.0 %gather_fusion = bf16[64,100,128]{2,1,0:T(8,128)(2,1)} fusion(bf16[32,100,128]{2,1,0:T(8,128)(2,1)S(1)} %copy.21, s32[1024]{0:T(1024)S(1)} %pad_clamp_fusion), kind=kCustom, calls=%fused_computation | custom fusion | bytes 3277056 | tf_op jit(solution)/shard_map/gather | solution.py:73
  39.4 0.9 %fusion.13 = (f32[512]{0:T(512)S(1)}, f32[4,1,512]{2,1,0:T(1,128)S(1)}) fusion(f16[4,193,512]{2,1,0:T(8,128)(2,1)} %all-to-all-done), kind=kLoop, calls=%fused_computation.46 | loop fusion | flops 7680 | bytes 14336 | tf_op jit(solution)/shard_map/reduce_min | solution.py:62
  40.3 1.3 %multiply_reduce_fusion = f32[192,512]{1,0:T(8,128)S(1)} fusion(f16[4,193,512]{2,1,0:T(8,128)(2,1)} %all-to-all-done, f32[4,512]{1,0:T(4,128)S(1)} %bitcast.81), kind=kLoop, calls=%fused_computation.3 | loop fusion | flops 1081344 | bytes 1187840 | tf_op jit(solution)/shard_map/reduce_sum | solution.py:61
  41.8 4.9 %collective-permute-start.5 = (f16[49,512]{1,0:T(8,128)(2,1)S(1)}, f16[49,512]{1,0:T(8,128)(2,1)S(1)}, u32[]{:S(2)}, u32[]{:S(2)}) collective-permute-start(f16[49,512]{1,0:T(8,128)(2,1)S(1)} %get-tuple-element.23), channel_id=1, source_target_pairs={{0,1},{1,2},{2,3},{3,0},{4,5},{5,6},{6,7},{7,4},{8,9},{9,10},{10,1... | collective-permute-start | bytes 150536 | tf_op jit(solution)/shard_map/ppermute | solution.py:67
  46.7 0.7 %fusion.2 = bf16[1,8,100,128]{3,2,1,0:T(8,128)(2,1)S(1)} fusion(bf16[8,8,100,128]{3,2,1,0:T(8,128)(2,1)S(1)} %bitcast.78, bf16[8,8,128,128]{3,2,1,0:T(8,128)(2,1)S(1)} %copy-done), kind=kOutput, calls=%fused_computation.9 | convolution fusion | flops 209817600 | bytes 3940352 | tf_op jit(solution)/shard_map/tbcx,tbxn->tcn/dot_general | solution.py:72
  47.4 0.7 %copy.26 = bf16[1,8,100,128]{3,1,2,0:T(8,128)(2,1)} copy(bf16[1,8,100,128]{3,2,1,0:T(8,128)(2,1)S(1)} %fusion.2) | data formatting | bytes 409600
  48.1 1.6 %collective-permute-start.6 = (f16[49,512]{1,0:T(8,128)(2,1)S(1)}, f16[49,512]{1,0:T(8,128)(2,1)S(1)}, u32[]{:S(2)}, u32[]{:S(2)}) collective-permute-start(f16[49,512]{1,0:T(8,128)(2,1)S(1)} %get-tuple-element.24), channel_id=1, source_target_pairs={{0,2},{1,3},{2,0},{3,1},{4,6},{5,7},{6,4},{7,5},{8,10},{9,11},{10,... | collective-permute-start | bytes 150536 | tf_op jit(solution)/shard_map/ppermute | solution.py:67
  49.7 0.8 %collective-permute-start.7 = (f16[49,512]{1,0:T(8,128)(2,1)S(1)}, f16[49,512]{1,0:T(8,128)(2,1)S(1)}, u32[]{:S(2)}, u32[]{:S(2)}) collective-permute-start(f16[49,512]{1,0:T(8,128)(2,1)S(1)} %get-tuple-element.25), channel_id=1, source_target_pairs={{0,3},{1,0},{2,1},{3,2},{4,7},{5,4},{6,5},{7,6},{8,11},{9,8},{10,9... | collective-permute-start | bytes 150536 | tf_op jit(solution)/shard_map/ppermute | solution.py:67
  50.5 3.4 %collective-permute-done.6 = f16[49,512]{1,0:T(8,128)(2,1)S(1)} collective-permute-done((f16[49,512]{1,0:T(8,128)(2,1)S(1)}, f16[49,512]{1,0:T(8,128)(2,1)S(1)}, u32[]{:S(2)}, u32[]{:S(2)}) %collective-permute-start.6) | collective-permute-done | bytes 50208 | tf_op jit(solution)/shard_map/ppermute | solution.py:67
  53.9 0.3 collective-permute-done.7
  54.2 0.7 %fusion.9 = f32[48,512]{1,0:T(8,128)} fusion(f32[4,48,512]{2,1,0:T(8,128)S(1)} %bitcast.80, s32[]{:T(128)S(6)} %select_n.95, f16[49,512]{1,0:T(8,128)(2,1)S(1)} %collective-permute-done.7, f16[49,512]{1,0:T(8,128)(2,1)S(1)} %collective-permute-done.6, f16[49,512]{1,0:T(8,128)(2,1)S(1)} %collective-permute-done.5, f32[512]{0:T(512)S(1)} %bitcast.85, ...), kind=kLoop, calls=%fused_computation.29 | loop fusion | flops 221184 | bytes 350212 | tf_op jit(solution)/shard_map/add | solution.py:67
  (34 shorter events, 0.3 us)
Async XLA Ops:
  0.6 46.0 %copy-start = (bf16[8,8,128,128]{3,2,1,0:T(8,128)(2,1)S(1)}, bf16[8,8,128,128]{3,2,1,0:T(8,128)(2,1)}, u32[]{:S(2)}) copy-start(bf16[8,8,128,128]{3,2,1,0:T(8,128)(2,1)} %param.10) | copy-start | bytes 6291460
  3.5 2.2 %copy-start.1 = (f32[4,192,512]{2,1,0:T(8,128)}, f32[4,192,512]{2,1,0:T(8,128)S(1)}, u32[]{:S(2)}) copy-start(f32[4,192,512]{2,1,0:T(8,128)S(1)} %fusion) | copy-start | bytes 4718596
  5.2 2.2 %copy-start.5 = (s32[1,4,8]{2,1,0:T(4,128)S(1)}, s32[1,4,8]{2,1,0:T(4,128)}, u32[]{:S(2)}) copy-start(s32[1,4,8]{2,1,0:T(4,128)} %param.8) | copy-start | bytes 388
  5.2 2.2 %copy-start.6 = (s32[1,4]{1,0:T(1,128)S(1)}, s32[1,4]{1,0:T(1,128)}, u32[]{:S(2)}) copy-start(s32[1,4]{1,0:T(1,128)} %param.9) | copy-start | bytes 52
  5.2 4.2 %collective-permute-start.3 = (f32[4,192,512]{2,1,0:T(8,128)}, f32[4,192,512]{2,1,0:T(8,128)}, u32[]{:S(2)}, u32[]{:S(2)}) collective-permute-start(f32[4,192,512]{2,1,0:T(8,128)} %select_bitcast_fusion), channel_id=1, source_target_pairs={{0,4},{4,0},{1,5},{5,1},{2,6},{6,2},{3,7},{7,3},{8,12},{12,8},{9,1... | collective-permute-start | bytes 4718600 | tf_op jit(solution)/shard_map/ppermute | solution.py:56
  7.3 2.1 %collective-permute-start.4 = (f32[1,512]{1,0:T(1,128)S(1)}, f32[1,512]{1,0:T(1,128)S(1)}, u32[]{:S(2)}, u32[]{:S(2)}) collective-permute-start(f32[1,512]{1,0:T(1,128)S(1)} %bitcast.86), channel_id=1, source_target_pairs={{0,4},{4,0},{1,5},{5,1},{2,6},{6,2},{3,7},{7,3},{8,12},{12,8},{9,1... | collective-permute-start | bytes 6152 | tf_op jit(solution)/shard_map/ppermute | solution.py:58
  7.4 2.0 %copy-start.2 = (f32[4,192,512]{2,1,0:T(8,128)S(1)}, f32[4,192,512]{2,1,0:T(8,128)}, u32[]{:S(2)}) copy-start(f32[4,192,512]{2,1,0:T(8,128)} %copy-done.1) | copy-start | bytes 4718596
  12.4 12.1 %copy-start.4 = (s32[8,8]{1,0:T(8,128)S(1)}, s32[8,8]{1,0:T(8,128)}, u32[]{:S(2)}) copy-start(s32[8,8]{1,0:T(8,128)} %param.11) | copy-start | bytes 772
  12.4 27.0 %all-to-all-start = ((f16[4,193,512]{2,1,0:T(8,128)(2,1)}), f16[4,193,512]{2,1,0:T(8,128)(2,1)}, u32[]{:S(2)}, u32[]{:S(2)}) async-start(f16[4,193,512]{2,1,0:T(8,128)(2,1)} %pad_maximum_fusion.1), calls=%async_computation | async-start | bytes 1638400 | tf_op jit(solution)/shard_map/all_to_all | solution.py:60
  18.4 10.4 %collective-permute-start = (bf16[8,100,128]{2,0,1:T(8,128)(2,1)}, bf16[8,100,128]{2,0,1:T(8,128)(2,1)S(1)}, u32[]{:S(2)}, u32[]{:S(2)}) collective-permute-start(bf16[8,100,128]{2,0,1:T(8,128)(2,1)} %get-tuple-element.19), channel_id=1, source_target_pairs={{0,1},{1,2},{2,3},{3,0},{4,5},{5,6},{6,7},{7,4},{8,9},{9,10},{10,1... | collective-permute-start | bytes 614408 | tf_op jit(solution)/shard_map/ppermute | solution.py:42
  20.5 16.4 %collective-permute-start.1 = (bf16[8,100,128]{2,0,1:T(8,128)(2,1)S(1)}, bf16[8,100,128]{2,0,1:T(8,128)(2,1)S(1)}, u32[]{:S(2)}, u32[]{:S(2)}) collective-permute-start(bf16[8,100,128]{2,0,1:T(8,128)(2,1)S(1)} %get-tuple-element.18), channel_id=1, source_target_pairs={{0,2},{1,3},{2,0},{3,1},{4,6},{5,7},{6,4},{7,5},{8,10},{9,11},{10,... | collective-permute-start | bytes 614408 | tf_op jit(solution)/shard_map/ppermute | solution.py:42
  23.1 13.8 %collective-permute-start.2 = (bf16[8,100,128]{2,0,1:T(8,128)(2,1)S(1)}, bf16[8,100,128]{2,0,1:T(8,128)(2,1)S(1)}, u32[]{:S(2)}, u32[]{:S(2)}) collective-permute-start(bf16[8,100,128]{2,0,1:T(8,128)(2,1)S(1)} %get-tuple-element.17), channel_id=1, source_target_pairs={{0,3},{1,0},{2,1},{3,2},{4,7},{5,4},{6,5},{7,6},{8,11},{9,8},{10,9... | collective-permute-start | bytes 614408 | tf_op jit(solution)/shard_map/ppermute | solution.py:42
  39.4 7.3 %copy-start.3 = (bf16[64,100,128]{2,1,0:T(8,128)(2,1)S(1)}, bf16[64,100,128]{2,1,0:T(8,128)(2,1)}, u32[]{:S(2)}) copy-start(bf16[64,100,128]{2,1,0:T(8,128)(2,1)} %gather_fusion) | copy-start | bytes 4915204
  41.8 8.7 %collective-permute-start.5 = (f16[49,512]{1,0:T(8,128)(2,1)S(1)}, f16[49,512]{1,0:T(8,128)(2,1)S(1)}, u32[]{:S(2)}, u32[]{:S(2)}) collective-permute-start(f16[49,512]{1,0:T(8,128)(2,1)S(1)} %get-tuple-element.23), channel_id=1, source_target_pairs={{0,1},{1,2},{2,3},{3,0},{4,5},{5,6},{6,7},{7,4},{8,9},{9,10},{10,1... | collective-permute-start | bytes 150536 | tf_op jit(solution)/shard_map/ppermute | solution.py:67
  48.1 5.8 %collective-permute-start.6 = (f16[49,512]{1,0:T(8,128)(2,1)S(1)}, f16[49,512]{1,0:T(8,128)(2,1)S(1)}, u32[]{:S(2)}, u32[]{:S(2)}) collective-permute-start(f16[49,512]{1,0:T(8,128)(2,1)S(1)} %get-tuple-element.24), channel_id=1, source_target_pairs={{0,2},{1,3},{2,0},{3,1},{4,6},{5,7},{6,4},{7,5},{8,10},{9,11},{10,... | collective-permute-start | bytes 150536 | tf_op jit(solution)/shard_map/ppermute | solution.py:67
  49.7 4.5 %collective-permute-start.7 = (f16[49,512]{1,0:T(8,128)(2,1)S(1)}, f16[49,512]{1,0:T(8,128)(2,1)S(1)}, u32[]{:S(2)}, u32[]{:S(2)}) collective-permute-start(f16[49,512]{1,0:T(8,128)(2,1)S(1)} %get-tuple-element.25), channel_id=1, source_target_pairs={{0,3},{1,0},{2,1},{3,2},{4,7},{5,4},{6,5},{7,6},{8,11},{9,8},{10,9... | collective-permute-start | bytes 150536 | tf_op jit(solution)/shard_map/ppermute | solution.py:67

commit v5 on v4

--- a/solution.py
+++ b/solution.py
@@ -38,9 +38,9 @@
     blocks = jnp.arange(sample.shape[0], dtype=jnp.int32)
     choose = (rolled[:, :, None] == blocks).astype(jnp.bfloat16)
     outgoing = jnp.einsum("kjb,bcx->kjcx", choose, sample, preferred_element_type=jnp.bfloat16)
-    incoming = [outgoing[0]] + [
-        lax.ppermute(outgoing[k], "sp", to_shift(k)) for k in range(1, shards)
-    ]
+    incoming = [outgoing[0]]
+    for k in range(1, shards):
+        incoming.append(lax.ppermute(outgoing[k], "sp", to_shift(k)))
 
     partial_grad = lax.dot_general(
         edge_inputs, cotangent, (((0,), (0,)), ((), ())), preferred_element_type=jnp.float32

time: 55.2 us -> 55.2 us (level)
  no operation moved by 1% of the time
where the time goes in v5:
time: 55.2 us; the launch traced here: 54.9 us
  starting transfers between devices  19.2 us (35%)
  waiting for transfers between devices  16 us (29%)
  other arithmetic  10 us (18%)
  matrix products  4.89 us (9%)
  local copies, waits for them, and re-layouts  3.9 us (7%)
  between operations  0.84 us (2%)
    ppermute x3, waiting for transfers between devices, work(): incoming.append(lax.ppermute(outgoing[k], 'sp', to_shift(k)))  12.3 us
    ppermute x3, starting transfers between devices, work(): lax.ppermute(pack(chunk, shift), 'sp', to_shift(k))  7.29 us
    ppermute x3, starting transfers between devices, work(): incoming.append(lax.ppermute(outgoing[k], 'sp', to_shift(k)))  6.02 us
    all_to_all x1, starting transfers between devices, work(): lax.all_to_all(packed, 'group', split_axis=0, concat_axis=0, tiled=True)  5.29 us
    ppermute x3, waiting for transfers between devices, work(): lax.ppermute(pack(chunk, shift), 'sp', to_shift(k))  3.67 us
    dot_general x1, matrix products, work(): lax.dot_general(edge_inputs, cotangent, (((0,), (0,)), ((), ())), preferr...  2.51 us
    gather x1, local copies, waits for them, and re-layouts, work(): block_pool[slot]  2 us
    convert_element_type x2, other arithmetic, pack(): scaled = (values * jnp.exp2(shift)).astype(jnp.float16)  1.86 us
  transfers between devices with their start and end apart: 9, of which 4 were waited for; matrix products, arithmetic and copies ran while one was open for 15% of the time, Pallas kernels for 0%

profile of v5, /device:TPU:0, one launch (start us, length us, event | category | flops | bytes accessed | tf_op | source)
XLA Modules:
  0.0 54.9 jit_solution(5851702114554271217)
XLA Ops:
  0.7 2.5 %fusion.29 = f32[1536,512]{1,0:T(8,128)S(1)} fusion(bf16[384,1536]{1,0:T(8,128)(2,1)} %param.12, bf16[384,512]{1,0:T(8,128)(2,1)} %param.13), kind=kOutput, calls=%fused_computation.78 | convolution fusion | flops 603979776 | bytes 4718592 | tf_op jit(solution)/shard_map/dot_general | solution.py:45
  3.2 0.4 fusion
  3.6 1.7 %select_bitcast_fusion = f32[4,192,512]{2,1,0:T(8,128)} fusion(f32[4,2,192,512]{3,2,1,0:T(8,128)S(1)} %bitcast.77, pred[]{:T(512)S(6)} %eq.48), kind=kLoop, calls=%fused_computation.6 | loop fusion | flops 393216 | bytes 4718593 | tf_op jit(solution)/shard_map/jit(_where)/select_n | solution.py:53
  5.2 0.5 collective-permute-start.3
  5.7 1.6 %maximum_reduce_fusion = f32[512]{0:T(512)S(1)} fusion(f32[4,192,512]{2,1,0:T(8,128)} %select_bitcast_fusion, f32[4,192,512]{2,1,0:T(8,128)S(1)} %fusion), kind=kLoop, calls=%fused_computation.5 | loop fusion | flops 1572352 | bytes 3147776 | tf_op jit(solution)/shard_map/reduce_max | solution.py:57
  7.3 0.1 collective-permute-start.4
  7.4 0.1 iota_compare_fusion.2
  7.5 0.1 select_reduce_fusion
  7.6 1.7 %fusion.3 = bf16[4,8,100,128]{3,1,2,0:T(8,128)(2,1)S(1)} fusion(bf16[1,32,100,128]{3,1,2,0:T(8,128)(2,1)} %param.7, s32[4,8]{1,0:T(4,128)S(1)} %select_reduce_fusion), kind=kOutput, calls=%fused_computation.12 | convolution fusion | flops 26215424 | bytes 1638528 | tf_op jit(solution)/shard_map/kjb,bcx->kjcx/dot_general | solution.py:40
  9.4 1.8 %multiply_convert_fusion = f16[4,192,512]{2,1,0:T(8,128)(2,1)S(1)} fusion(f32[4,192,512]{2,1,0:T(8,128)S(1)} %copy-done.2, f32[4,192,512]{2,1,0:T(8,128)} %collective-permute-done.3, f32[512]{0:T(512)S(1)} %bitcast.82), kind=kLoop, calls=%fused_computation.4 | loop fusion | flops 1179648 | bytes 3934208 | tf_op jit(solution)/shard_map/convert_element_type | solution.py:12
  11.2 1.1 %pad_maximum_fusion.1 = f16[4,193,512]{2,1,0:T(8,128)(2,1)} fusion(f16[4,1,512]{2,1,0:T(2,128)(2,1)S(1)} %broadcast_in_dim.57, f16[4,192,512]{2,1,0:T(8,128)(2,1)S(1)} %multiply_convert_fusion), kind=kLoop, calls=%fused_computation.11 | loop fusion | flops 395264 | bytes 1581056 | tf_op jit(solution)/shard_map/concatenate | solution.py:14
  12.4 5.3 %all-to-all-start = ((f16[4,193,512]{2,1,0:T(8,128)(2,1)}), f16[4,193,512]{2,1,0:T(8,128)(2,1)}, u32[]{:S(2)}, u32[]{:S(2)}) async-start(f16[4,193,512]{2,1,0:T(8,128)(2,1)} %pad_maximum_fusion.1), calls=%async_computation | async-start | bytes 1638400 | tf_op jit(solution)/shard_map/all_to_all | solution.py:60
  17.6 0.7 %slice_bitcast_fusion.3 = (bf16[8,100,128]{2,0,1:T(8,128)(2,1)S(1)}, bf16[8,100,128]{2,0,1:T(8,128)(2,1)S(1)}, bf16[8,100,128]{2,0,1:T(8,128)(2,1)S(1)}, bf16[8,100,128]{2,0,1:T(8,128)(2,1)}) fusion(bf16[4,8,100,128]{3,1,2,0:T(8,128)(2,1)S(1)} %fusion.3), kind=kLoop, calls=%fused_computation.17 | loop fusion | bytes 1638400 | tf_op jit(solution)/shard_map/squeeze | solution.py:41
  18.4 2.1 %collective-permute-start = (bf16[8,100,128]{2,0,1:T(8,128)(2,1)}, bf16[8,100,128]{2,0,1:T(8,128)(2,1)S(1)}, u32[]{:S(2)}, u32[]{:S(2)}) collective-permute-start(bf16[8,100,128]{2,0,1:T(8,128)(2,1)} %get-tuple-element.19), channel_id=1, source_target_pairs={{0,1},{1,2},{2,3},{3,0},{4,5},{5,6},{6,7},{7,4},{8,9},{9,10},{10,1... | collective-permute-start | bytes 614408 | tf_op jit(solution)/shard_map/ppermute | solution.py:43
  20.5 2.6 %collective-permute-start.1 = (bf16[8,100,128]{2,0,1:T(8,128)(2,1)S(1)}, bf16[8,100,128]{2,0,1:T(8,128)(2,1)S(1)}, u32[]{:S(2)}, u32[]{:S(2)}) collective-permute-start(bf16[8,100,128]{2,0,1:T(8,128)(2,1)S(1)} %get-tuple-element.18), channel_id=1, source_target_pairs={{0,2},{1,3},{2,0},{3,1},{4,6},{5,7},{6,4},{7,5},{8,10},{9,11},{10,... | collective-permute-start | bytes 614408 | tf_op jit(solution)/shard_map/ppermute | solution.py:43
  23.1 1.3 %collective-permute-start.2 = (bf16[8,100,128]{2,0,1:T(8,128)(2,1)S(1)}, bf16[8,100,128]{2,0,1:T(8,128)(2,1)S(1)}, u32[]{:S(2)}, u32[]{:S(2)}) collective-permute-start(bf16[8,100,128]{2,0,1:T(8,128)(2,1)S(1)} %get-tuple-element.17), channel_id=1, source_target_pairs={{0,3},{1,0},{2,1},{3,2},{4,7},{5,4},{6,5},{7,6},{8,11},{9,8},{10,9... | collective-permute-start | bytes 614408 | tf_op jit(solution)/shard_map/ppermute | solution.py:43
  24.5 0.1 reshape.132
  24.6 4.2 %collective-permute-done = bf16[8,100,128]{2,0,1:T(8,128)(2,1)S(1)} collective-permute-done((bf16[8,100,128]{2,0,1:T(8,128)(2,1)}, bf16[8,100,128]{2,0,1:T(8,128)(2,1)S(1)}, u32[]{:S(2)}, u32[]{:S(2)}) %collective-permute-start) | collective-permute-done | bytes 204832 | tf_op jit(solution)/shard_map/ppermute | solution.py:43
  28.8 8.1 %collective-permute-done.1 = bf16[8,100,128]{2,0,1:T(8,128)(2,1)S(1)} collective-permute-done((bf16[8,100,128]{2,0,1:T(8,128)(2,1)S(1)}, bf16[8,100,128]{2,0,1:T(8,128)(2,1)S(1)}, u32[]{:S(2)}, u32[]{:S(2)}) %collective-permute-start.1) | collective-permute-done | bytes 204832 | tf_op jit(solution)/shard_map/ppermute | solution.py:43
  36.9 0.1 pad_maximum_fusion
  37.0 0.3 copy.21
  37.4 2.0 %gather_fusion = bf16[64,100,128]{2,1,0:T(8,128)(2,1)} fusion(bf16[32,100,128]{2,1,0:T(8,128)(2,1)S(1)} %copy.21, s32[1024]{0:T(1024)S(1)} %pad_clamp_fusion), kind=kCustom, calls=%fused_computation | custom fusion | bytes 3277056 | tf_op jit(solution)/shard_map/gather | solution.py:73
  39.4 0.9 %fusion.13 = (f32[512]{0:T(512)S(1)}, f32[4,1,512]{2,1,0:T(1,128)S(1)}) fusion(f16[4,193,512]{2,1,0:T(8,128)(2,1)} %all-to-all-done), kind=kLoop, calls=%fused_computation.46 | loop fusion | flops 7680 | bytes 14336 | tf_op jit(solution)/shard_map/reduce_min | solution.py:62
  40.3 1.3 %multiply_reduce_fusion = f32[192,512]{1,0:T(8,128)S(1)} fusion(f16[4,193,512]{2,1,0:T(8,128)(2,1)} %all-to-all-done, f32[4,512]{1,0:T(4,128)S(1)} %bitcast.81), kind=kLoop, calls=%fused_computation.3 | loop fusion | flops 1081344 | bytes 1187840 | tf_op jit(solution)/shard_map/reduce_sum | solution.py:61
  41.8 4.9 %collective-permute-start.5 = (f16[49,512]{1,0:T(8,128)(2,1)S(1)}, f16[49,512]{1,0:T(8,128)(2,1)S(1)}, u32[]{:S(2)}, u32[]{:S(2)}) collective-permute-start(f16[49,512]{1,0:T(8,128)(2,1)S(1)} %get-tuple-element.23), channel_id=1, source_target_pairs={{0,1},{1,2},{2,3},{3,0},{4,5},{5,6},{6,7},{7,4},{8,9},{9,10},{10,1... | collective-permute-start | bytes 150536 | tf_op jit(solution)/shard_map/ppermute | solution.py:67
  46.7 0.7 %fusion.2 = bf16[1,8,100,128]{3,2,1,0:T(8,128)(2,1)S(1)} fusion(bf16[8,8,100,128]{3,2,1,0:T(8,128)(2,1)S(1)} %bitcast.78, bf16[8,8,128,128]{3,2,1,0:T(8,128)(2,1)S(1)} %copy-done), kind=kOutput, calls=%fused_computation.9 | convolution fusion | flops 209817600 | bytes 3940352 | tf_op jit(solution)/shard_map/tbcx,tbxn->tcn/dot_general | solution.py:72
  47.4 0.7 %copy.26 = bf16[1,8,100,128]{3,1,2,0:T(8,128)(2,1)} copy(bf16[1,8,100,128]{3,2,1,0:T(8,128)(2,1)S(1)} %fusion.2) | data formatting | bytes 409600
  48.1 1.6 %collective-permute-start.6 = (f16[49,512]{1,0:T(8,128)(2,1)S(1)}, f16[49,512]{1,0:T(8,128)(2,1)S(1)}, u32[]{:S(2)}, u32[]{:S(2)}) collective-permute-start(f16[49,512]{1,0:T(8,128)(2,1)S(1)} %get-tuple-element.24), channel_id=1, source_target_pairs={{0,2},{1,3},{2,0},{3,1},{4,6},{5,7},{6,4},{7,5},{8,10},{9,11},{10,... | collective-permute-start | bytes 150536 | tf_op jit(solution)/shard_map/ppermute | solution.py:67
  49.7 0.8 %collective-permute-start.7 = (f16[49,512]{1,0:T(8,128)(2,1)S(1)}, f16[49,512]{1,0:T(8,128)(2,1)S(1)}, u32[]{:S(2)}, u32[]{:S(2)}) collective-permute-start(f16[49,512]{1,0:T(8,128)(2,1)S(1)} %get-tuple-element.25), channel_id=1, source_target_pairs={{0,3},{1,0},{2,1},{3,2},{4,7},{5,4},{6,5},{7,6},{8,11},{9,8},{10,9... | collective-permute-start | bytes 150536 | tf_op jit(solution)/shard_map/ppermute | solution.py:67
  50.5 3.4 %collective-permute-done.6 = f16[49,512]{1,0:T(8,128)(2,1)S(1)} collective-permute-done((f16[49,512]{1,0:T(8,128)(2,1)S(1)}, f16[49,512]{1,0:T(8,128)(2,1)S(1)}, u32[]{:S(2)}, u32[]{:S(2)}) %collective-permute-start.6) | collective-permute-done | bytes 50208 | tf_op jit(solution)/shard_map/ppermute | solution.py:67
  53.9 0.3 collective-permute-done.7
  54.2 0.7 %fusion.9 = f32[48,512]{1,0:T(8,128)} fusion(f32[4,48,512]{2,1,0:T(8,128)S(1)} %bitcast.80, s32[]{:T(128)S(6)} %select_n.95, f16[49,512]{1,0:T(8,128)(2,1)S(1)} %collective-permute-done.7, f16[49,512]{1,0:T(8,128)(2,1)S(1)} %collective-permute-done.6, f16[49,512]{1,0:T(8,128)(2,1)S(1)} %collective-permute-done.5, f32[512]{0:T(512)S(1)} %bitcast.85, ...), kind=kLoop, calls=%fused_computation.29 | loop fusion | flops 221184 | bytes 350212 | tf_op jit(solution)/shard_map/add | solution.py:67
  (34 shorter events, 0.3 us)
Async XLA Ops:
  0.6 46.0 %copy-start = (bf16[8,8,128,128]{3,2,1,0:T(8,128)(2,1)S(1)}, bf16[8,8,128,128]{3,2,1,0:T(8,128)(2,1)}, u32[]{:S(2)}) copy-start(bf16[8,8,128,128]{3,2,1,0:T(8,128)(2,1)} %param.10) | copy-start | bytes 6291460
  3.5 2.2 %copy-start.1 = (f32[4,192,512]{2,1,0:T(8,128)}, f32[4,192,512]{2,1,0:T(8,128)S(1)}, u32[]{:S(2)}) copy-start(f32[4,192,512]{2,1,0:T(8,128)S(1)} %fusion) | copy-start | bytes 4718596
  5.2 2.2 %copy-start.5 = (s32[1,4,8]{2,1,0:T(4,128)S(1)}, s32[1,4,8]{2,1,0:T(4,128)}, u32[]{:S(2)}) copy-start(s32[1,4,8]{2,1,0:T(4,128)} %param.8) | copy-start | bytes 388
  5.2 2.2 %copy-start.6 = (s32[1,4]{1,0:T(1,128)S(1)}, s32[1,4]{1,0:T(1,128)}, u32[]{:S(2)}) copy-start(s32[1,4]{1,0:T(1,128)} %param.9) | copy-start | bytes 52
  5.2 4.2 %collective-permute-start.3 = (f32[4,192,512]{2,1,0:T(8,128)}, f32[4,192,512]{2,1,0:T(8,128)}, u32[]{:S(2)}, u32[]{:S(2)}) collective-permute-start(f32[4,192,512]{2,1,0:T(8,128)} %select_bitcast_fusion), channel_id=1, source_target_pairs={{0,4},{4,0},{1,5},{5,1},{2,6},{6,2},{3,7},{7,3},{8,12},{12,8},{9,1... | collective-permute-start | bytes 4718600 | tf_op jit(solution)/shard_map/ppermute | solution.py:56
  7.3 2.1 %collective-permute-start.4 = (f32[1,512]{1,0:T(1,128)S(1)}, f32[1,512]{1,0:T(1,128)S(1)}, u32[]{:S(2)}, u32[]{:S(2)}) collective-permute-start(f32[1,512]{1,0:T(1,128)S(1)} %bitcast.86), channel_id=1, source_target_pairs={{0,4},{4,0},{1,5},{5,1},{2,6},{6,2},{3,7},{7,3},{8,12},{12,8},{9,1... | collective-permute-start | bytes 6152 | tf_op jit(solution)/shard_map/ppermute | solution.py:58
  7.4 2.0 %copy-start.2 = (f32[4,192,512]{2,1,0:T(8,128)S(1)}, f32[4,192,512]{2,1,0:T(8,128)}, u32[]{:S(2)}) copy-start(f32[4,192,512]{2,1,0:T(8,128)} %copy-done.1) | copy-start | bytes 4718596
  12.4 12.1 %copy-start.4 = (s32[8,8]{1,0:T(8,128)S(1)}, s32[8,8]{1,0:T(8,128)}, u32[]{:S(2)}) copy-start(s32[8,8]{1,0:T(8,128)} %param.11) | copy-start | bytes 772
  12.4 27.0 %all-to-all-start = ((f16[4,193,512]{2,1,0:T(8,128)(2,1)}), f16[4,193,512]{2,1,0:T(8,128)(2,1)}, u32[]{:S(2)}, u32[]{:S(2)}) async-start(f16[4,193,512]{2,1,0:T(8,128)(2,1)} %pad_maximum_fusion.1), calls=%async_computation | async-start | bytes 1638400 | tf_op jit(solution)/shard_map/all_to_all | solution.py:60
  18.4 10.4 %collective-permute-start = (bf16[8,100,128]{2,0,1:T(8,128)(2,1)}, bf16[8,100,128]{2,0,1:T(8,128)(2,1)S(1)}, u32[]{:S(2)}, u32[]{:S(2)}) collective-permute-start(bf16[8,100,128]{2,0,1:T(8,128)(2,1)} %get-tuple-element.19), channel_id=1, source_target_pairs={{0,1},{1,2},{2,3},{3,0},{4,5},{5,6},{6,7},{7,4},{8,9},{9,10},{10,1... | collective-permute-start | bytes 614408 | tf_op jit(solution)/shard_map/ppermute | solution.py:43
  20.5 16.4 %collective-permute-start.1 = (bf16[8,100,128]{2,0,1:T(8,128)(2,1)S(1)}, bf16[8,100,128]{2,0,1:T(8,128)(2,1)S(1)}, u32[]{:S(2)}, u32[]{:S(2)}) collective-permute-start(bf16[8,100,128]{2,0,1:T(8,128)(2,1)S(1)} %get-tuple-element.18), channel_id=1, source_target_pairs={{0,2},{1,3},{2,0},{3,1},{4,6},{5,7},{6,4},{7,5},{8,10},{9,11},{10,... | collective-permute-start | bytes 614408 | tf_op jit(solution)/shard_map/ppermute | solution.py:43
  23.1 13.8 %collective-permute-start.2 = (bf16[8,100,128]{2,0,1:T(8,128)(2,1)S(1)}, bf16[8,100,128]{2,0,1:T(8,128)(2,1)S(1)}, u32[]{:S(2)}, u32[]{:S(2)}) collective-permute-start(bf16[8,100,128]{2,0,1:T(8,128)(2,1)S(1)} %get-tuple-element.17), channel_id=1, source_target_pairs={{0,3},{1,0},{2,1},{3,2},{4,7},{5,4},{6,5},{7,6},{8,11},{9,8},{10,9... | collective-permute-start | bytes 614408 | tf_op jit(solution)/shard_map/ppermute | solution.py:43
  39.4 7.3 %copy-start.3 = (bf16[64,100,128]{2,1,0:T(8,128)(2,1)S(1)}, bf16[64,100,128]{2,1,0:T(8,128)(2,1)}, u32[]{:S(2)}) copy-start(bf16[64,100,128]{2,1,0:T(8,128)(2,1)} %gather_fusion) | copy-start | bytes 4915204
  41.8 8.7 %collective-permute-start.5 = (f16[49,512]{1,0:T(8,128)(2,1)S(1)}, f16[49,512]{1,0:T(8,128)(2,1)S(1)}, u32[]{:S(2)}, u32[]{:S(2)}) collective-permute-start(f16[49,512]{1,0:T(8,128)(2,1)S(1)} %get-tuple-element.23), channel_id=1, source_target_pairs={{0,1},{1,2},{2,3},{3,0},{4,5},{5,6},{6,7},{7,4},{8,9},{9,10},{10,1... | collective-permute-start | bytes 150536 | tf_op jit(solution)/shard_map/ppermute | solution.py:67
  48.1 5.8 %collective-permute-start.6 = (f16[49,512]{1,0:T(8,128)(2,1)S(1)}, f16[49,512]{1,0:T(8,128)(2,1)S(1)}, u32[]{:S(2)}, u32[]{:S(2)}) collective-permute-start(f16[49,512]{1,0:T(8,128)(2,1)S(1)} %get-tuple-element.24), channel_id=1, source_target_pairs={{0,2},{1,3},{2,0},{3,1},{4,6},{5,7},{6,4},{7,5},{8,10},{9,11},{10,... | collective-permute-start | bytes 150536 | tf_op jit(solution)/shard_map/ppermute | solution.py:67
  49.7 4.5 %collective-permute-start.7 = (f16[49,512]{1,0:T(8,128)(2,1)S(1)}, f16[49,512]{1,0:T(8,128)(2,1)S(1)}, u32[]{:S(2)}, u32[]{:S(2)}) collective-permute-start(f16[49,512]{1,0:T(8,128)(2,1)S(1)} %get-tuple-element.25), channel_id=1, source_target_pairs={{0,3},{1,0},{2,1},{3,2},{4,7},{5,4},{6,5},{7,6},{8,11},{9,8},{10,9... | collective-permute-start | bytes 150536 | tf_op jit(solution)/shard_map/ppermute | solution.py:67
